TPU v7x, 256 devices: a whole 4x4x8 slice. The times are simulated.
256 devices in a mesh: grp: 8 (over x, core), mem: 32 (over y, z).
Axes of the slice: x: 4, y: 4, z: 8, core: 2. Of those that a mesh axis runs over, the one named last changes fastest.
Arguments:
- features: bfloat16 [262144, 4096], P(('grp', 'mem')), may hold values from -0.09375 to 0.09375
- re_features: bfloat16 [262144, 256], P(('grp', 'mem')), may hold values from -6 to 6
- member_id: int32 [262144], P(('grp', 'mem')), may hold values from 0 to 2047, as said below
- slot: int32 [262144], P(('grp', 'mem')), may hold values from 0 to 2047, as said below
- labels: int32 [262144], P(('grp', 'mem')), may hold values 0 or 1
- offsets: float32 [262144], P(('grp', 'mem')), may hold values from -6 to 6
- feature_scale: float32 [4096], replicated, may hold values from 0.3 to 3
- w_start: float32 [4096], replicated, may hold values from -4 to 4
Outputs:
- fixed_weights: float32 [4096], replicated
- member_coef: float32 [2048, 256], P(('grp', 'mem'))
- row_offsets: float32 [262144], P(('grp', 'mem'))
Inputs may be any that keep to these rules, and one draw needn't show every extreme that they name: A row of device k (devices counted along grp, then mem) belongs to group k // 32: member_id // 256 is that group, and (member_id mod 256) // 8 equals slot // 64. Rows per member are uneven. Within one device's rows the slots are distinct; slot // 64 is the mem index that owns the row's member, so at most 64 rows of one device go to one owner, and in every group one owner receives exactly 64 rows from every device of the group.
All inputs are finite; a program needn't handle non-finite values. No bound on the sum of `labels` on one device may be relied on, other than what follows from the above.
Results may differ from a plain program's by a relative error of at most 0.0003.
Values may be sent and summed in bfloat16 or wider, within the bound.
No kernel may reach another device: no remote copies, remote signals or barrier semaphores. Data moves between devices by JAX's collectives and lax.ppermute only.
A program may use at most 64 MiB of HBM per device.

v0:
```python
import functools
import jax
import jax.numpy as jnp
from jax import lax
from jax.experimental import pallas as pl
from jax.experimental.pallas import tpu as pltpu
from jax.sharding import Mesh, PartitionSpec as P

MEM_DEV = 8
NEWTON = 2
RIDGE = 1.0
PANEL = 16
BLOCK = 8
STEPS = 4
F32 = jnp.float32
BF16 = jnp.bfloat16
HIGH = lax.Precision.HIGHEST


def dot_nn(a, b, precision=None):
    return lax.dot_general(a, b, (((1,), (0,)), ((), ())), precision=precision,
                           preferred_element_type=F32)


def dot_nt(a, b, precision=None):
    return lax.dot_general(a, b, (((1,), (1,)), ((), ())), precision=precision,
                           preferred_element_type=F32)


def dot_tn(a, b, precision=None):
    return lax.dot_general(a, b, (((0,), (0,)), ((), ())), precision=precision,
                           preferred_element_type=F32)


def split_rows(row):
    high = row.astype(BF16).astype(F32)
    low = row - high
    at = lax.broadcasted_iota(jnp.int32, (8, row.shape[1]), 0)
    return jnp.where(at == 0, high, jnp.where(at == 1, low, 0.0)).astype(BF16)


def sigmoid(x):
    return 1.0 / (1.0 + jnp.exp(-x))


def total(row):
    return jnp.sum(row, axis=1, keepdims=True)


def sum_parts(ref):
    acc = ref[0]
    for i in range(1, ref.shape[0]):
        acc = acc + ref[i]
    return acc


def forward(xs, x_ref, xs_ref, row_ref, arrive=None):
    xs_ref[...] = xs
    block = x_ref.shape[0] // STEPS

    def body(i, carry):
        at = pl.multiple_of(i * block, block)
        if arrive is not None:
            arrive(i, at, block)
        both = dot_nt(xs_ref[...], x_ref[pl.ds(at, block), :])
        row_ref[:, pl.ds(at, block)] = both[0:1] + both[1:2]
        return carry

    lax.fori_loop(0, STEPS, body, 0)
    return row_ref[...]


def backward(row, x_ref, split_ref, out_ref):
    split_ref[...] = split_rows(row)
    block = x_ref.shape[1] // STEPS

    def body(i, carry):
        at = pl.multiple_of(i * block, block)
        both = dot_nn(split_ref[...], x_ref[:, pl.ds(at, block)])
        val = both[0:1] + both[1:2]
        for j in range(out_ref.shape[0]):
            out_ref[j, :, pl.ds(at, block)] = val
        return carry

    lax.fori_loop(0, STEPS, body, 0)


def start_kernel(x_hbm, z_hbm, slot_hbm, member_hbm, lab_hbm, off_hbm, scale_hbm, w_hbm,
                 packed_ref, x_ref, slot_ref, code_ref, lab_ref, off_ref, scale_ref, w_ref,
                 out_ref, score_ref, curv_ref,
                 z_ref, member_ref, int_ref, buf, xs_ref, split_ref, sems, xsems, psems):
    pairs = [(slot_hbm, slot_ref), (z_hbm, z_ref), (scale_hbm, scale_ref), (w_hbm, w_ref),
             (member_hbm, member_ref), (lab_hbm, int_ref), (off_hbm, off_ref)]
    loads = [pltpu.make_async_copy(src, dst, sems.at[i]) for i, (src, dst) in enumerate(pairs)]
    for load in loads:
        load.start()

    def chunk(i, at, block):
        return pltpu.make_async_copy(x_hbm.at[pl.ds(at, block)], x_ref.at[pl.ds(at, block)],
                                     xsems.at[i])

    block = x_ref.shape[0] // STEPS
    for i in range(STEPS):
        chunk(i, i * block, block).start()
    loads[0].wait()
    loads[1].wait()
    size = buf.shape[1]
    stores = []
    for b in range(buf.shape[0]):
        rows = lax.broadcasted_iota(jnp.int32, (size, slot_ref.shape[1]), 0) + b * size
        hot = jnp.where(rows == slot_ref[...], 1.0, 0.0).astype(BF16)
        buf[b] = dot_nn(hot, z_ref[...]).astype(BF16)
        stores.append(pltpu.make_async_copy(
            buf.at[b], packed_ref.at[pl.ds(b * size, size)], psems.at[b]))
        stores[-1].start()
    for load in loads[2:]:
        load.wait()
    labels = int_ref[...]
    lab_ref[...] = labels.astype(F32)
    code_ref[...] = (member_ref[...] % MEM_DEV + 8 * labels + 16).astype(F32)
    score = forward(split_rows(scale_ref[...] * w_ref[...]), x_ref, xs_ref, score_ref,
                    lambda i, at, size: chunk(i, at, size).wait())
    prob = sigmoid(score + off_ref[...])
    curv_ref[...] = prob * (1.0 - prob)
    backward(prob - lab_ref[...], x_ref, split_ref, out_ref)
    for store in stores:
        store.wait()


def grad_next_kernel(x_ref, part_ref, rr_ref, w_ref, u_ref, p_ref, score_ref, t_ref, m_ref,
                     off_ref, lab_ref, out_ref, w_out, score_out, curv_ref, xs_ref, split_ref):
    a = last_coef(part_ref, rr_ref, p_ref)
    w_out[...] = w_ref[...] + (u_ref[...] + a * p_ref[...])
    score = score_ref[...] + (m_ref[...] + a * t_ref[...])
    prob = sigmoid(score + off_ref[...])
    score_out[...] = score
    curv_ref[...] = prob * (1.0 - prob)
    backward(prob - lab_ref[...], x_ref, split_ref, out_ref)


def last_coef(part_ref, rr_ref, p_ref):
    p = p_ref[...]
    php = jnp.sum(part_ref[:, 0, :], axis=0, keepdims=True)[:, 0:1] + RIDGE * total(p * p)
    return rr_ref[:, 0:1] / php


def cg_first_kernel(x_ref, sum_ref, scale_ref, w_ref, curv_ref, out_ref, p_out, rr_out, t_ref,
                    xs_ref, split_ref):
    r = -(scale_ref[...] * sum_parts(sum_ref) + RIDGE * w_ref[...])
    p_out[...] = r
    rr_out[...] = jnp.broadcast_to(total(r * r), rr_out.shape)
    t = forward(split_rows(scale_ref[...] * r), x_ref, xs_ref, t_ref)
    backward(curv_ref[...] * t, x_ref, split_ref, out_ref)


def cg_update(sum_ref, scale_ref, p_ref, r_ref, u_ref, rr_ref, p_out, r_out, u_out, rr_out):
    p = p_ref[...]
    q = scale_ref[...] * sum_parts(sum_ref) + RIDGE * p
    rr = rr_ref[:, 0:1]
    a = rr / total(p * q)
    u = a * p if u_ref is None else u_ref[...] + a * p
    r = r_ref[...] - a * q
    nn = total(r * r)
    p = r + (nn / rr) * p
    u_out[...] = u
    if r_out is not None:
        r_out[...] = r
    p_out[...] = p
    rr_out[...] = jnp.broadcast_to(nn, rr_out.shape)
    return a, split_rows(scale_ref[...] * p)


def cg_next_kernel(x_ref, sum_ref, scale_ref, curv_ref, p_ref, rr_ref, t_in,
                   out_ref, p_out, r_out, u_out, rr_out, t_ref, m_ref, xs_ref, split_ref):
    a, xs = cg_update(sum_ref, scale_ref, p_ref, p_ref, None, rr_ref, p_out, r_out, u_out, rr_out)
    m_ref[...] = a * t_in[...]
    t = forward(xs, x_ref, xs_ref, t_ref)
    backward(curv_ref[...] * t, x_ref, split_ref, out_ref)


def cg_last_kernel(x_ref, sum_ref, scale_ref, curv_ref, p_ref, r_ref, u_ref, rr_ref, t_in, m_in,
                   out_ref, p_out, u_out, rr_out, t_ref, m_ref, xs_ref, split_ref):
    a, xs = cg_update(sum_ref, scale_ref, p_ref, r_ref, u_ref, rr_ref, p_out, None, u_out, rr_out)
    m_ref[...] = m_in[...] + a * t_in[...]
    t = forward(xs, x_ref, xs_ref, t_ref)
    out_ref[...] = jnp.broadcast_to(total(curv_ref[...] * t * t).reshape(1, 1, 1), out_ref.shape)


def owner_hot(slot, owners, cap):
    rows = lax.broadcasted_iota(jnp.int32, (owners, slot.shape[1]), 0)
    hot_owner = jnp.where(rows == slot // cap, 1.0, 0.0)
    lanes = lax.broadcasted_iota(jnp.int32, (cap, slot.shape[1]), 0)
    hot_cap = jnp.where(lanes == slot % cap, 1.0, 0.0)
    return hot_owner, hot_cap


def cg_last_pack_kernel(x_ref, sum_ref, scale_ref, curv_ref, p_ref, r_ref, u_ref, rr_ref, t_in,
                        m_in, score_ref, slot_ref, code_ref, out_ref, p_out, u_out, rr_out,
                        t_ref, xs_ref, split_ref):
    a, xs = cg_update(sum_ref, scale_ref, p_ref, r_ref, u_ref, rr_ref, p_out, None, u_out, rr_out)
    owners, cap = out_ref.shape[0], out_ref.shape[2] // 4
    hot_owner, hot_cap = owner_hot(slot_ref[...], owners, cap)
    t = forward(xs, x_ref, xs_ref, t_ref)
    done = score_ref[...] + (m_in[...] + a * t_in[...])
    php = total(curv_ref[...] * t * t)
    left = jnp.concatenate([hot_owner * done, hot_owner * t, hot_owner * code_ref[...]], axis=0)
    send = dot_nt(left, hot_cap, HIGH)
    part = jnp.broadcast_to(php, (1, cap))
    for i in range(owners):
        out_ref[i] = jnp.concatenate(
            [send[j * owners + i:j * owners + i + 1] for j in range(3)] + [part], axis=1)


def again_kernel(sum_ref, out_ref):
    val = sum_parts(sum_ref)
    for i in range(out_ref.shape[0]):
        out_ref[i] = val


def part_kernel(arr_ref, out_ref):
    last = arr_ref.shape[2] - 1
    got = arr_ref[:, 0, :]
    val = jnp.sum(got, axis=0, keepdims=True)[:, last:]
    out_ref[...] = jnp.broadcast_to(val.reshape(1, 1, 1), out_ref.shape)


def three_parts(v):
    a = v.astype(BF16)
    rest = v - a.astype(F32)
    b = rest.astype(BF16)
    c = (rest - b.astype(F32)).astype(BF16)
    return a, b, c


def get_lanes(halves, rows, lane):
    if lane:
        return halves[1][rows, :]
    return jnp.concatenate([halves[0][rows, :], halves[1][rows, :]], axis=1)


def put_lanes(halves, rows, lane, value):
    if lane:
        halves[1][rows, :] = value
    else:
        halves[0][rows, :] = value[:, :128]
        halves[1][rows, :] = value[:, 128:]


def reduce_block(rows, lane, block, others):
    def at(i, j):
        return jnp.broadcast_to(rows[i][0][:, lane + j:lane + j + 1], rows[i][0].shape)

    block, others = list(block), list(others)
    c = {(i, j): at(i, j) for i in block for j in block if j <= i}
    far = {(i, j): at(i, j) for i in others for j in block}
    lower, inv = {}, {}
    for j in block:
        inv[j] = 1.0 / c[j, j]
        for i in block:
            if i > j:
                lower[i, j] = c[i, j] * inv[j]
        for i in block:
            for k in block:
                if j < k <= i:
                    c[i, k] = c[i, k] - lower[i, j] * c[k, j]
    for j in block:
        for i in block:
            if i > j:
                rows[i] = [v - lower[i, j] * w for v, w in zip(rows[i], rows[j])]
    for j in block:
        rows[j] = [w * inv[j] for w in rows[j]]
    for j in reversed(block):
        for i in block:
            if i < j:
                rows[i] = [v - lower[j, i] * w for v, w in zip(rows[i], rows[j])]
    for j in block:
        for i in others:
            rows[i] = [v - far[i, j] * w for v, w in zip(rows[i], rows[j])]


def member_kernel(z_hbm, arr_ref, part_ref, rr_ref, w_ref, u_ref, p_ref,
                  w_out, coef_ref, back_ref,
                  base, tvec, code, zt, hi, lo, mat0, mat1, red0, red1, z_ref, sem):
    copy = pltpu.make_async_copy(z_hbm, z_ref, sem)
    copy.start()
    owners = arr_ref.shape[0]
    cap = arr_ref.shape[2] // 4
    fr = z_ref.shape[1]
    slots = z_ref.shape[0]
    p = p_ref[...]
    php = jnp.sum(part_ref[:, 0, :], axis=0, keepdims=True)[:, 0:1] + RIDGE * total(p * p)
    a = rr_ref[:, 0:1] / php
    w_out[...] = w_ref[...] + (u_ref[...] + a * p)
    for o in range(owners):
        got = arr_ref[o]
        base[:, o * cap:(o + 1) * cap] = got[:, 0:cap]
        tvec[:, o * cap:(o + 1) * cap] = got[:, cap:2 * cap]
        code[:, o * cap:(o + 1) * cap] = got[:, 2 * cap:3 * cap]
    prob = sigmoid(base[...] + a * tvec[...])
    curv = prob * (1.0 - prob)
    codes = code[...]
    label = jnp.where(codes >= 24.0, 1.0, 0.0)
    resid = prob - label
    local = codes - 16.0 - 8.0 * label
    at = lax.broadcasted_iota(jnp.int32, (MEM_DEV, slots), 0).astype(F32)
    onehot = jnp.where(local == at, 1.0, 0.0)

    copy.wait()
    z_t = z_ref[...].T
    zt[...] = z_t
    chunk = 512
    for c in range(0, slots, chunk):
        cz = zt[:, c:c + chunk].astype(F32) * curv[:, c:c + chunk]
        high = cz.astype(BF16)
        hi[:, c:c + chunk] = high
        lo[:, c:c + chunk] = (cz - high.astype(F32)).astype(BF16)
    mat, red = (mat0, mat1), (red0, red1)
    eye = jnp.where(lax.broadcasted_iota(jnp.int32, (fr, fr), 0)
                    == lax.broadcasted_iota(jnp.int32, (fr, fr), 1), RIDGE, 0.0)
    for m in range(MEM_DEV):
        mask = onehot[m:m + 1].astype(BF16)
        gram = dot_nn(hi[...] * mask, z_ref[...]) + dot_nn(lo[...] * mask, z_ref[...])
        put_lanes(mat, slice(m * fr, (m + 1) * fr), 0, gram + eye)
    rm = resid * onehot
    rm_high = rm.astype(BF16)
    rm_low = (rm - rm_high.astype(F32)).astype(BF16)
    rhs = dot_nn(rm_high, z_ref[...]) + dot_nn(rm_low, z_ref[...])

    for k0 in range(0, fr, PANEL):
        lane0 = (k0 // 128) * 128
        orig = [get_lanes(mat, pl.ds(k0 + i, MEM_DEV, stride=fr), lane0) for i in range(PANEL)]
        wide = (MEM_DEV, 128)
        rows = [[o[:, c:c + 128] for c in range(0, o.shape[1], 128)]
                + [jnp.broadcast_to(rhs[:, k0 + i:k0 + i + 1], wide)]
                for i, o in enumerate(orig)]
        reduce_block(rows, k0 - lane0, range(BLOCK), range(BLOCK, PANEL))
        reduce_block(rows, k0 - lane0, range(BLOCK, PANEL), range(BLOCK))
        ys = [jnp.concatenate([r[-1]] * (len(r) - 1), axis=1) for r in rows]
        rows = [r[0] if len(r) == 2 else jnp.concatenate(r[:-1], axis=1) for r in rows]
        tail = rhs[:, lane0:]
        lanes = lax.broadcasted_iota(jnp.int32, tail.shape, 1) + lane0
        drop = jnp.zeros_like(tail)
        place = tail
        for i in range(PANEL):
            drop = drop + orig[i] * ys[i]
            place = jnp.where(lanes == k0 + i, ys[i], place)
        tail = jnp.where(lanes >= k0 + PANEL, tail - drop, place)
        rhs = tail if lane0 == 0 else jnp.concatenate([rhs[:, :lane0], tail], axis=1)
        for i in range(PANEL):
            put_lanes(red, slice((k0 + i) * MEM_DEV, (k0 + i + 1) * MEM_DEV), lane0, rows[i])
        top = k0 + PANEL
        if top < fr:
            lane1 = (top // 128) * 128
            row1 = lane1
            for m in range(MEM_DEV):
                o = get_lanes(mat, slice(m * fr + k0, m * fr + k0 + PANEL), row1)
                w = get_lanes(red, pl.ds(k0 * MEM_DEV + m, PANEL, stride=MEM_DEV), lane1)
                o1, o2, o3 = three_parts(o)
                w1, w2, w3 = three_parts(w)
                left = jnp.concatenate([o1, o1, o2, o2, o1, o3], axis=0)
                right = jnp.concatenate([w1, w2, w1, w2, w3, w1], axis=0)
                rest = slice(m * fr + row1, (m + 1) * fr)
                put_lanes(mat, rest, lane1, get_lanes(mat, rest, lane1) - dot_tn(left, right))

    lanes = lax.broadcasted_iota(jnp.int32, rhs.shape, 1)
    sol = jnp.where(lanes >= fr - PANEL, rhs, 0.0)
    for k0 in range(fr - 2 * PANEL, -1, -PANEL):
        new = sol
        lane0 = (k0 // 128) * 128
        for i in range(PANEL):
            w = get_lanes(red, slice((k0 + i) * MEM_DEV, (k0 + i + 1) * MEM_DEV), lane0)
            d = jnp.sum(w * sol[:, lane0:], axis=1, keepdims=True)
            new = jnp.where(lanes == k0 + i, rhs - d, new)
        sol = new
    coef = -sol
    coef_ref[...] = coef
    chigh = coef.astype(BF16)
    clow = (coef - chigh.astype(F32)).astype(BF16)
    scores = dot_nn(chigh, zt[...]) + dot_nn(clow, zt[...])
    back = jnp.sum(scores * onehot, axis=0, keepdims=True)
    for o in range(owners):
        back_ref[o] = back[:, o * cap:(o + 1) * cap]


def unpack_kernel(back_ref, slot_ref, out_ref):
    owners, _, cap = back_ref.shape
    back = back_ref[:, 0, :]
    hot_owner, hot_cap = owner_hot(slot_ref[...], owners, cap)
    rows = dot_tn(back, hot_owner, HIGH)
    out_ref[...] = jnp.sum(rows * hot_cap, axis=0, keepdims=True)


VMEM_LIMIT = 32 * 1024 * 1024
STAGE_LIMIT = 20 * 1024 * 1024


def on_chip(kernel, name, outs, *ins, scratch=()):
    vmem = pl.BlockSpec(memory_space=pltpu.VMEM)
    return pl.pallas_call(
        kernel,
        in_specs=[vmem] * len(ins),
        out_specs=[vmem] * len(outs),
        out_shape=[jax.ShapeDtypeStruct(s, d) for s, d in outs],
        scratch_shapes=list(scratch),
        compiler_params=pltpu.CompilerParams(vmem_limit_bytes=STAGE_LIMIT),
        name=name,
    )(*ins)


PH1 = ("core", "z")
PH2 = ("x", "y")


def on_device(features, re_features, member_id, slot, labels, offsets, feature_scale, w_start,
              *, sizes):
    n1 = sizes["core"] * sizes["z"]
    n2 = sizes["x"] * sizes["y"]
    n_mem = sizes["y"] * sizes["z"]
    n_grp = sizes["x"] * sizes["core"]
    rows, f = features.shape
    fr = re_features.shape[1]
    slots = 2 * rows
    cap = slots // n_mem
    def exchange(v, axes):
        return lax.all_to_all(v, axes, 0, 0, tiled=True)

    def reduce_rest(parts):
        got = exchange(parts, PH1)
        mid, = on_chip(again_kernel, "again", [((n2, 1, f), F32)], got)
        return exchange(mid, PH2)

    tmp = [pltpu.VMEM((8, f), BF16), pltpu.VMEM((8, rows), BF16)]
    vec = ((1, f), F32)
    small = ((1, 128), F32)
    row = ((1, rows), F32)
    parts = ((n1, 1, f), F32)
    vmem = pl.BlockSpec(memory_space=pltpu.VMEM)
    hbm = pl.BlockSpec(memory_space=pltpu.HBM)
    outs = [((rows, f), BF16), ((1, rows), jnp.int32), row, row, row, vec, vec, parts, row, row]
    packed, x, slot_row, code, lab, off, scale, w, gpart, score, curv = pl.pallas_call(
        start_kernel,
        in_specs=[hbm] * 8,
        out_specs=[hbm] + [vmem] * len(outs),
        out_shape=[pltpu.HBM((slots, fr), BF16)] + [jax.ShapeDtypeStruct(*o) for o in outs],
        scratch_shapes=[pltpu.VMEM((rows, fr), BF16)] + [pltpu.VMEM((1, rows), jnp.int32)] * 2
        + [pltpu.VMEM((8, slots // 8, fr), BF16)] + tmp
        + [pltpu.SemaphoreType.DMA((7,)), pltpu.SemaphoreType.DMA((STEPS,)),
           pltpu.SemaphoreType.DMA((8,))],
        compiler_params=pltpu.CompilerParams(vmem_limit_bytes=STAGE_LIMIT),
        name="start",
    )(*[pltpu.with_memory_space_constraint(v, pltpu.HBM) for v in (
        features, re_features, slot.reshape(1, rows), member_id.reshape(1, rows),
        labels.reshape(1, rows), offsets.reshape(1, rows), feature_scale.reshape(1, f),
        w_start.reshape(1, f))])
    z_got = lax.all_to_all(packed.reshape(n_mem, cap, fr), ("y", "z"), 0, 0, tiled=True)
    z_got = z_got.reshape(slots, fr)
    for it in range(NEWTON):
        g2 = reduce_rest(gpart)
        hpart, p, rr, t = on_chip(cg_first_kernel, "cg_first", [parts, vec, small, row],
                                  x, g2, scale, w, curv, scratch=tmp)
        h2 = reduce_rest(hpart)
        if it == 0:
            h2, z_got = lax.optimization_barrier((h2, z_got))
        hpart, p, r, u, rr, t, m = on_chip(
            cg_next_kernel, "cg_next", [parts, vec, vec, vec, small, row, row],
            x, h2, scale, curv, p, rr, t, scratch=tmp)
        h2 = reduce_rest(hpart)
        ins = (x, h2, scale, curv, p, r, u, rr, t, m)
        if it + 1 < NEWTON:
            spart, p, u, rr, t, m = on_chip(
                cg_last_kernel, "cg_last", [((n1 * n2, 1, 128), F32), vec, vec, small, row, row],
                *ins, scratch=tmp)
            sgot = exchange(spart, ("x", "core", "y", "z"))
            gpart, w, score, curv = on_chip(
                grad_next_kernel, "grad_next", [parts, vec, row, row],
                x, sgot, rr, w, u, p, score, t, m, off, lab, scratch=tmp)
        else:
            send, p, u, rr = on_chip(
                cg_last_pack_kernel, "cg_last_pack",
                [((n_mem, 1, 4 * cap), F32), vec, vec, small],
                *ins, score, slot_row, code, scratch=[pltpu.VMEM((1, rows), F32)] + tmp)
    got = exchange(send, ("y", "z"))
    part, = on_chip(part_kernel, "part", [((n_grp, 1, 128), F32)], got)
    part = exchange(part, ("x", "core"))
    z_got = pltpu.with_memory_space_constraint(z_got, pltpu.HBM)
    w, member_coef, back = pl.pallas_call(
        member_kernel,
        in_specs=[pl.BlockSpec(memory_space=pltpu.HBM)] + [vmem] * 6,
        out_shape=[jax.ShapeDtypeStruct((1, f), F32),
                   jax.ShapeDtypeStruct((MEM_DEV, fr), F32),
                   jax.ShapeDtypeStruct((n_mem, 1, cap), F32)],
        scratch_shapes=[pltpu.VMEM((1, slots), F32)] * 3
        + [pltpu.VMEM((fr, slots), BF16)] * 3
        + [pltpu.VMEM((MEM_DEV * fr, 128), F32)] * 4
        + [pltpu.VMEM((slots, fr), BF16), pltpu.SemaphoreType.DMA(())],
        compiler_params=pltpu.CompilerParams(vmem_limit_bytes=VMEM_LIMIT),
        name="members",
    )(z_got, got, part, rr, w, u, p)
    returned = exchange(back, ("y", "z"))
    row_offsets = pl.pallas_call(
        unpack_kernel,
        out_shape=jax.ShapeDtypeStruct((1, rows), F32),
        compiler_params=pltpu.CompilerParams(vmem_limit_bytes=VMEM_LIMIT),
        name="unpack",
    )(returned, slot_row)
    return (w.reshape(f), member_coef, row_offsets.reshape(rows))


def solution(mesh):
    n_grp, n_mem = mesh.shape["grp"], mesh.shape["mem"]
    shape = {"x": n_grp // 2, "core": 2, "y": 4, "z": n_mem // 4}
    fine = Mesh(mesh.devices.reshape(tuple(shape.values())), tuple(shape))
    cut = P(("x", "core", "y", "z"))
    cut2 = P(("x", "core", "y", "z"), None)
    return jax.shard_map(
        functools.partial(on_device, sizes=shape),
        mesh=fine,
        in_specs=(cut2, cut2, cut, cut, cut, cut, P(), P()),
        out_specs=(P(), cut2, cut),
        check_vma=False,
    )
```

profile of v0, /device:TPU:1, one launch (start us, length us, event | category | flops | bytes accessed | tf_op | source)
XLA Modules:
  0.0 311.0 jit_solution(16274821615621962040)
XLA Ops:
  0.6 7.7 %start.1 = (bf16[2048,256]{1,0:T(8,128)(2,1)}, bf16[1024,4096]{1,0:T(8,128)(2,1)S(1)}, s32[1,1024]{1,0:T(1,128)S(1)}, f32[1,1024]{1,0:T(1,128)S(1)}, f32[1,1024]...) custom-call(bf16[1024,4096]{1,0:T(8,128)(2,1)} %x_hbm.1, ...), custom_call_target="tpu_custom_call" | custom-call | tf_op jit(solution)/shard_map/start/pallas_call | solution.py:440
  8.4 19.3 %all_to_all.85.sum_ref = f32[16,1,4096]{2,1,0:T(1,128)S(1)} all-to-all(f32[16,1,4096]{2,1,0:T(1,128)S(1)} %get-tuple-element.56), channel_id=1, replica_groups=mesh['x'=4,'core'=2,'y'=4,'z'=8] {'core','z'}, dimensions={0} | all-to-all | bytes 524288 | tf_op jit(solution)/shard_map/all_to_all | solution.py:425
  27.7 13.9 %all_to_all.86.sum_ref = f32[16,1,4096]{2,1,0:T(1,128)S(1)} all-to-all(f32[16,1,4096]{2,1,0:T(1,128)S(1)} %again.6), channel_id=1, replica_groups=mesh['x'=4,'core'=2,'y'=4,'z'=8] {'x','y'}, dimensions={0} | all-to-all | bytes 524288 | tf_op jit(solution)/shard_map/all_to_all | solution.py:425
  41.6 4.4 %cg_first.2 = (f32[16,1,4096]{2,1,0:T(1,128)S(1)}, f32[1,4096]{1,0:T(1,128)S(1)}, f32[1,128]{1,0:T(1,128)S(1)}, f32[1,1024]{1,0:T(1,128)S(1)}) custom-call(bf16[1024,4096]{1,0:T(8,128)(2,1)S(1)} %get-tuple-element.55.x_ref, f32[16,1,4096]{2,1,0:T(1,128)S(1)} %all_to_all.86.sum_ref, f32[1,4096]{1,0:T(1,128)S(1)} %get-tuple-element.57.scale_ref, ...), custom_call_target="tpu_custom_call" | custom-call | tf_op jit(solution)/shard_map/cg_first/pallas_call | solution.py:399
  46.0 16.0 %all_to_all.87.sum_ref = f32[16,1,4096]{2,1,0:T(1,128)S(1)} all-to-all(f32[16,1,4096]{2,1,0:T(1,128)S(1)} %get-tuple-element.60), channel_id=1, replica_groups=mesh['x'=4,'core'=2,'y'=4,'z'=8] {'core','z'}, dimensions={0} | all-to-all | bytes 524288 | tf_op jit(solution)/shard_map/all_to_all | solution.py:425
  62.1 10.5 %all_to_all.88.sum_ref = f32[16,1,4096]{2,1,0:T(1,128)S(1)} all-to-all(f32[16,1,4096]{2,1,0:T(1,128)S(1)} %again.7), channel_id=1, replica_groups=mesh['x'=4,'core'=2,'y'=4,'z'=8] {'x','y'}, dimensions={0} | all-to-all | bytes 524288 | tf_op jit(solution)/shard_map/all_to_all | solution.py:425
  72.6 31.2 %all_to_all.89 = bf16[32,64,256]{2,1,0:T(8,128)(2,1)} all-to-all(bf16[32,64,256]{2,1,0:T(8,128)(2,1)S(1)} %bitcast.11), channel_id=1, replica_groups=mesh['x'=4,'core'=2,'y'=4,'z'=8] {'y','z'}, dimensions={0} | all-to-all | bytes 2097152 | tf_op jit(solution)/shard_map/all_to_all | solution.py:455
  103.7 4.7 %cg_next.2 = (f32[16,1,4096]{2,1,0:T(1,128)S(1)}, f32[1,4096]{1,0:T(1,128)S(1)}, f32[1,4096]{1,0:T(1,128)S(1)}, f32[1,4096]{1,0:T(1,128)S(1)}, f32[1,128]{1,0:T(...) custom-call(bf16[1024,4096]{1,0:T(8,128)(2,1)S(1)} %get-tuple-element.55.x_ref, ...), custom_call_target="tpu_custom_call" | custom-call | tf_op jit(solution)/shard_map/cg_next/pallas_call | solution.py:399
  108.4 17.8 %all_to_all.90.sum_ref = f32[16,1,4096]{2,1,0:T(1,128)S(1)} all-to-all(f32[16,1,4096]{2,1,0:T(1,128)S(1)} %get-tuple-element.67), channel_id=1, replica_groups=mesh['x'=4,'core'=2,'y'=4,'z'=8] {'core','z'}, dimensions={0} | all-to-all | bytes 524288 | tf_op jit(solution)/shard_map/all_to_all | solution.py:425
  126.2 10.5 %all_to_all.91.sum_ref = f32[16,1,4096]{2,1,0:T(1,128)S(1)} all-to-all(f32[16,1,4096]{2,1,0:T(1,128)S(1)} %again.8), channel_id=1, replica_groups=mesh['x'=4,'core'=2,'y'=4,'z'=8] {'x','y'}, dimensions={0} | all-to-all | bytes 524288 | tf_op jit(solution)/shard_map/all_to_all | solution.py:425
  140.0 22.0 %all_to_all.92.part_ref = f32[256,1,128]{2,1,0:T(1,128)S(1)} all-to-all(f32[256,1,128]{2,1,0:T(1,128)S(1)} %get-tuple-element.74), channel_id=1, replica_groups=mesh['x'=4,'core'=2,'y'=4,'z'=8] {'x','core','y','z'}, dimensions={0} | all-to-all | bytes 262144 | tf_op jit(solution)/shard_map/all_to_all | solution.py:425
  163.8 12.4 %all_to_all.93.sum_ref = f32[16,1,4096]{2,1,0:T(1,128)S(1)} all-to-all(f32[16,1,4096]{2,1,0:T(1,128)S(1)} %get-tuple-element.83), channel_id=1, replica_groups=mesh['x'=4,'core'=2,'y'=4,'z'=8] {'core','z'}, dimensions={0} | all-to-all | bytes 524288 | tf_op jit(solution)/shard_map/all_to_all | solution.py:425
  176.3 10.3 %all_to_all.94.sum_ref = f32[16,1,4096]{2,1,0:T(1,128)S(1)} all-to-all(f32[16,1,4096]{2,1,0:T(1,128)S(1)} %again.9), channel_id=1, replica_groups=mesh['x'=4,'core'=2,'y'=4,'z'=8] {'x','y'}, dimensions={0} | all-to-all | bytes 524288 | tf_op jit(solution)/shard_map/all_to_all | solution.py:425
  186.6 4.4 %cg_first.3 = (f32[16,1,4096]{2,1,0:T(1,128)S(1)}, f32[1,4096]{1,0:T(1,128)S(1)}, f32[1,128]{1,0:T(1,128)S(1)}, f32[1,1024]{1,0:T(1,128)S(1)}) custom-call(bf16[1024,4096]{1,0:T(8,128)(2,1)S(1)} %get-tuple-element.55.x_ref, f32[16,1,4096]{2,1,0:T(1,128)S(1)} %all_to_all.94.sum_ref, f32[1,4096]{1,0:T(1,128)S(1)} %get-tuple-element.57.scale_ref, ...), custom_call_target="tpu_custom_call" | custom-call | tf_op jit(solution)/shard_map/cg_first/pallas_call | solution.py:399
  191.0 16.0 %all_to_all.95.sum_ref = f32[16,1,4096]{2,1,0:T(1,128)S(1)} all-to-all(f32[16,1,4096]{2,1,0:T(1,128)S(1)} %get-tuple-element.86), channel_id=1, replica_groups=mesh['x'=4,'core'=2,'y'=4,'z'=8] {'core','z'}, dimensions={0} | all-to-all | bytes 524288 | tf_op jit(solution)/shard_map/all_to_all | solution.py:425
  207.1 10.5 %all_to_all.96.sum_ref = f32[16,1,4096]{2,1,0:T(1,128)S(1)} all-to-all(f32[16,1,4096]{2,1,0:T(1,128)S(1)} %again.10), channel_id=1, replica_groups=mesh['x'=4,'core'=2,'y'=4,'z'=8] {'x','y'}, dimensions={0} | all-to-all | bytes 524288 | tf_op jit(solution)/shard_map/all_to_all | solution.py:425
  217.6 4.7 %cg_next.3 = (f32[16,1,4096]{2,1,0:T(1,128)S(1)}, f32[1,4096]{1,0:T(1,128)S(1)}, f32[1,4096]{1,0:T(1,128)S(1)}, f32[1,4096]{1,0:T(1,128)S(1)}, f32[1,128]{1,0:T(...) custom-call(bf16[1024,4096]{1,0:T(8,128)(2,1)S(1)} %get-tuple-element.55.x_ref, ...), custom_call_target="tpu_custom_call" | custom-call | tf_op jit(solution)/shard_map/cg_next/pallas_call | solution.py:399
  222.3 16.0 %all_to_all.97.sum_ref = f32[16,1,4096]{2,1,0:T(1,128)S(1)} all-to-all(f32[16,1,4096]{2,1,0:T(1,128)S(1)} %get-tuple-element.90), channel_id=1, replica_groups=mesh['x'=4,'core'=2,'y'=4,'z'=8] {'core','z'}, dimensions={0} | all-to-all | bytes 524288 | tf_op jit(solution)/shard_map/all_to_all | solution.py:425
  238.4 10.5 %all_to_all.98.sum_ref = f32[16,1,4096]{2,1,0:T(1,128)S(1)} all-to-all(f32[16,1,4096]{2,1,0:T(1,128)S(1)} %again.11), channel_id=1, replica_groups=mesh['x'=4,'core'=2,'y'=4,'z'=8] {'x','y'}, dimensions={0} | all-to-all | bytes 524288 | tf_op jit(solution)/shard_map/all_to_all | solution.py:425
  248.8 3.7 %cg_last_pack.1 = (f32[32,1,256]{2,1,0:T(1,128)S(1)}, f32[1,4096]{1,0:T(1,128)S(1)}, f32[1,4096]{1,0:T(1,128)S(1)}, f32[1,128]{1,0:T(1,128)S(1)}) custom-call(bf16[1024,4096]{1,0:T(8,128)(2,1)S(1)} %get-tuple-element.55.x_ref, f32[16,1,4096]{2,1,0:T(1,128)S(1)} %all_to_all.98.sum_ref, f32[1,4096]{1,0:T(1,128)S(1)} %get-tuple-element.57.scale_ref, ...), custom_call_target="tpu_custom_call" | custom-call | tf_op jit(solution)/shard_map/cg_last_pack/pallas_call | solution.py:399
  252.6 15.1 %all_to_all.99.arr_ref = f32[32,1,256]{2,1,0:T(1,128)S(1)} all-to-all(f32[32,1,256]{2,1,0:T(1,128)S(1)} %get-tuple-element.100), channel_id=1, replica_groups=mesh['x'=4,'core'=2,'y'=4,'z'=8] {'y','z'}, dimensions={0} | all-to-all | bytes 65536 | tf_op jit(solution)/shard_map/all_to_all | solution.py:425
  267.8 9.7 %all_to_all.100.part_ref = f32[8,1,128]{2,1,0:T(1,128)S(1)} all-to-all(f32[8,1,128]{2,1,0:T(1,128)S(1)} %part.1), channel_id=1, replica_groups=mesh['x'=4,'core'=2,'y'=4,'z'=8] {'x','core'}, dimensions={0} | all-to-all | bytes 8192 | tf_op jit(solution)/shard_map/all_to_all | solution.py:425
  277.5 20.9 %members.1 = (f32[1,4096]{1,0:T(1,128)}, f32[8,256]{1,0:T(8,128)}, f32[32,1,64]{2,1,0:T(1,128)S(1)}) custom-call(bf16[2048,256]{1,0:T(8,128)(2,1)} %bitcast.10, f32[32,1,256]{2,1,0:T(1,128)S(1)} %all_to_all.99.arr_ref, f32[8,1,128]{2,1,0:T(1,128)S(1)} %all_to_all.100.part_ref, f32[1,128]{1,0:T(1,128)S(1)} %get-tuple-element.101.rr_ref, ...), custom_call_target="tpu_custom_call" | custom-call | tf_op jit(solution)/shard_map/members/pallas_call | solution.py:486
  298.3 11.6 %all_to_all.101.back_ref = f32[32,1,64]{2,1,0:T(1,128)S(1)} all-to-all(f32[32,1,64]{2,1,0:T(1,128)S(1)} %get-tuple-element.106), channel_id=1, replica_groups=mesh['x'=4,'core'=2,'y'=4,'z'=8] {'y','z'}, dimensions={0} | all-to-all | bytes 16384 | tf_op jit(solution)/shard_map/all_to_all | solution.py:425
  (12 shorter events, 6.4 us)
Async XLA Ops:
  8.3 64.2 %copy-start = (bf16[2048,256]{1,0:T(8,128)(2,1)S(1)}, bf16[2048,256]{1,0:T(8,128)(2,1)}, u32[]{:S(2)}) copy-start(bf16[2048,256]{1,0:T(8,128)(2,1)} %get-tuple-element.61) | copy-start | bytes 3145732
where the time goes:
time: 312 us; the launch traced here: 311 us
  blocking collectives  253 us (81%)
  Pallas kernels  57 us (18%)
    all_to_all x16, blocking collectives, exchange(): return lax.all_to_all(v, axes, 0, 0, tiled=True)  222 us
    all_to_all x1, blocking collectives, on_device(): lax.all_to_all(packed.reshape(n_mem, cap, fr), ('y', 'z'), 0, 0, tiled=True)  31.2 us
    pallas_call x14, Pallas kernels, on_chip(): pl.pallas_call(kernel, in_specs=[vmem] * len(ins), out_specs=[vmem] * len...  27.4 us
    pallas_call x1, Pallas kernels, on_device(): pl.pallas_call(member_kernel, in_specs=[pl.BlockSpec(memory_space=pltpu.H...  20.9 us
    pallas_call x1, Pallas kernels, on_device(): pl.pallas_call(start_kernel, in_specs=[hbm] * 8, out_specs=[hbm] + [vmem]...  7.71 us

commit v1 on v0

--- a/solution.py
+++ b/solution.py
@@ -12,6 +12,8 @@
 PANEL = 16
 BLOCK = 8
 STEPS = 4
+UNROLL = 4
+GRAM_UNROLL = 1
 F32 = jnp.float32
 BF16 = jnp.bfloat16
 HIGH = lax.Precision.HIGHEST
@@ -86,9 +88,9 @@
 
 
 def start_kernel(x_hbm, z_hbm, slot_hbm, member_hbm, lab_hbm, off_hbm, scale_hbm, w_hbm,
-                 packed_ref, x_ref, slot_ref, code_ref, lab_ref, off_ref, scale_ref, w_ref,
+                 packed_ref, slot_ref, code_ref, lab_ref, off_ref, scale_ref, w_ref,
                  out_ref, score_ref, curv_ref,
-                 z_ref, member_ref, int_ref, buf, xs_ref, split_ref, sems, xsems, psems):
+                 x_ref, z_ref, member_ref, int_ref, buf, xs_ref, split_ref, sems, xsems, psems):
     pairs = [(slot_hbm, slot_ref), (z_hbm, z_ref), (scale_hbm, scale_ref), (w_hbm, w_ref),
              (member_hbm, member_ref), (lab_hbm, int_ref), (off_hbm, off_ref)]
     loads = [pltpu.make_async_copy(src, dst, sems.at[i]) for i, (src, dst) in enumerate(pairs)]
@@ -145,12 +147,25 @@
 
 
 def cg_first_kernel(x_ref, sum_ref, scale_ref, w_ref, curv_ref, out_ref, p_out, rr_out, t_ref,
-                    xs_ref, split_ref):
+                    xs_ref, split_ref, arrive=None):
     r = -(scale_ref[...] * sum_parts(sum_ref) + RIDGE * w_ref[...])
     p_out[...] = r
     rr_out[...] = jnp.broadcast_to(total(r * r), rr_out.shape)
-    t = forward(split_rows(scale_ref[...] * r), x_ref, xs_ref, t_ref)
+    t = forward(split_rows(scale_ref[...] * r), x_ref, xs_ref, t_ref, arrive)
     backward(curv_ref[...] * t, x_ref, split_ref, out_ref)
+
+
+def cg_load_kernel(x_hbm, sum_ref, scale_ref, w_ref, curv_ref, x_ref, out_ref, p_out, rr_out,
+                   t_ref, xs_ref, split_ref, sems):
+    def chunk(i, at, block):
+        return pltpu.make_async_copy(x_hbm.at[pl.ds(at, block)], x_ref.at[pl.ds(at, block)],
+                                     sems.at[i])
+
+    block = x_ref.shape[0] // STEPS
+    for i in range(STEPS):
+        chunk(i, i * block, block).start()
+    cg_first_kernel(x_ref, sum_ref, scale_ref, w_ref, curv_ref, out_ref, p_out, rr_out, t_ref,
+                    xs_ref, split_ref, lambda i, at, size: chunk(i, at, size).wait())
 
 
 def cg_update(sum_ref, scale_ref, p_ref, r_ref, u_ref, rr_ref, p_out, r_out, u_out, rr_out):
@@ -215,6 +230,10 @@
     val = sum_parts(sum_ref)
     for i in range(out_ref.shape[0]):
         out_ref[i] = val
+
+
+def add_four_kernel(a_ref, b_ref, c_ref, d_ref, out_ref):
+    out_ref[...] = (a_ref[...] + b_ref[...]) + (c_ref[...] + d_ref[...])
 
 
 def part_kernel(arr_ref, out_ref):
@@ -280,7 +299,7 @@
 
 def member_kernel(z_hbm, arr_ref, part_ref, rr_ref, w_ref, u_ref, p_ref,
                   w_out, coef_ref, back_ref,
-                  base, tvec, code, zt, hi, lo, mat0, mat1, red0, red1, z_ref, sem):
+                  base, tvec, code, zt, hi, lo, mat0, mat1, red0, red1, z_ref, hot_ref, sem):
     copy = pltpu.make_async_copy(z_hbm, z_ref, sem)
     copy.start()
     owners = arr_ref.shape[0]
@@ -317,10 +336,15 @@
     mat, red = (mat0, mat1), (red0, red1)
     eye = jnp.where(lax.broadcasted_iota(jnp.int32, (fr, fr), 0)
                     == lax.broadcasted_iota(jnp.int32, (fr, fr), 1), RIDGE, 0.0)
-    for m in range(MEM_DEV):
-        mask = onehot[m:m + 1].astype(BF16)
+    hot_ref[...] = onehot
+
+    def one_gram(m, carry):
+        mask = hot_ref[pl.ds(m, 1), :].astype(BF16)
         gram = dot_nn(hi[...] * mask, z_ref[...]) + dot_nn(lo[...] * mask, z_ref[...])
-        put_lanes(mat, slice(m * fr, (m + 1) * fr), 0, gram + eye)
+        put_lanes(mat, pl.ds(pl.multiple_of(m * fr, fr), fr), 0, gram + eye)
+        return carry
+
+    lax.fori_loop(0, MEM_DEV, one_gram, 0, unroll=GRAM_UNROLL)
     rm = resid * onehot
     rm_high = rm.astype(BF16)
     rm_low = (rm - rm_high.astype(F32)).astype(BF16)
@@ -352,15 +376,19 @@
         if top < fr:
             lane1 = (top // 128) * 128
             row1 = lane1
-            for m in range(MEM_DEV):
-                o = get_lanes(mat, slice(m * fr + k0, m * fr + k0 + PANEL), row1)
+            def trailing(m, carry, k0=k0, row1=row1, lane1=lane1):
+                first = pl.multiple_of(m * fr, fr)
+                o = get_lanes(mat, pl.ds(first + k0, PANEL), row1)
                 w = get_lanes(red, pl.ds(k0 * MEM_DEV + m, PANEL, stride=MEM_DEV), lane1)
                 o1, o2, o3 = three_parts(o)
                 w1, w2, w3 = three_parts(w)
                 left = jnp.concatenate([o1, o1, o2, o2, o1, o3], axis=0)
                 right = jnp.concatenate([w1, w2, w1, w2, w3, w1], axis=0)
-                rest = slice(m * fr + row1, (m + 1) * fr)
+                rest = pl.ds(first + row1, fr - row1)
                 put_lanes(mat, rest, lane1, get_lanes(mat, rest, lane1) - dot_tn(left, right))
+                return carry
+
+            lax.fori_loop(0, MEM_DEV, trailing, 0, unroll=UNROLL)
 
     lanes = lax.broadcasted_iota(jnp.int32, rhs.shape, 1)
     sol = jnp.where(lanes >= fr - PANEL, rhs, 0.0)
@@ -429,6 +457,22 @@
         mid, = on_chip(again_kernel, "again", [((n2, 1, f), F32)], got)
         return exchange(mid, PH2)
 
+    def reduce_permutes(v):
+        half = sizes["z"] // 2
+        def flip(index, size):
+            return [(i, index(i)) for i in range(size)]
+        nz = sizes["z"]
+        phases = [
+            ("x", sizes["x"], [lambda i, b=b: i ^ b for b in (1, 2, 3)]),
+            ("y", sizes["y"], [lambda i, b=b: i ^ b for b in (1, 2, 3)]),
+            (("core", "z"), n1, [lambda i, b=b: i ^ b for b in (nz, half, nz + half)]),
+            ("z", nz, [lambda i, b=b: i ^ b for b in (1, 2, 3)]),
+        ]
+        for axes, size, maps in phases:
+            moved = [lax.ppermute(v, axes, flip(index, size)) for index in maps]
+            v, = on_chip(add_four_kernel, "add_four", [((1, 1, f), F32)], v, *moved)
+        return v
+
     tmp = [pltpu.VMEM((8, f), BF16), pltpu.VMEM((8, rows), BF16)]
     vec = ((1, f), F32)
     small = ((1, 128), F32)
@@ -436,13 +480,14 @@
     parts = ((n1, 1, f), F32)
     vmem = pl.BlockSpec(memory_space=pltpu.VMEM)
     hbm = pl.BlockSpec(memory_space=pltpu.HBM)
-    outs = [((rows, f), BF16), ((1, rows), jnp.int32), row, row, row, vec, vec, parts, row, row]
-    packed, x, slot_row, code, lab, off, scale, w, gpart, score, curv = pl.pallas_call(
+    outs = [((1, rows), jnp.int32), row, row, row, vec, vec,
+            ((1, 1, f), F32), row, row]
+    packed, slot_row, code, lab, off, scale, w, gpart, score, curv = pl.pallas_call(
         start_kernel,
         in_specs=[hbm] * 8,
         out_specs=[hbm] + [vmem] * len(outs),
         out_shape=[pltpu.HBM((slots, fr), BF16)] + [jax.ShapeDtypeStruct(*o) for o in outs],
-        scratch_shapes=[pltpu.VMEM((rows, fr), BF16)] + [pltpu.VMEM((1, rows), jnp.int32)] * 2
+        scratch_shapes=[pltpu.VMEM((rows, f), BF16), pltpu.VMEM((rows, fr), BF16)] + [pltpu.VMEM((1, rows), jnp.int32)] * 2
         + [pltpu.VMEM((8, slots // 8, fr), BF16)] + tmp
         + [pltpu.SemaphoreType.DMA((7,)), pltpu.SemaphoreType.DMA((STEPS,)),
            pltpu.SemaphoreType.DMA((8,))],
@@ -455,12 +500,25 @@
     z_got = lax.all_to_all(packed.reshape(n_mem, cap, fr), ("y", "z"), 0, 0, tiled=True)
     z_got = z_got.reshape(slots, fr)
     for it in range(NEWTON):
-        g2 = reduce_rest(gpart)
-        hpart, p, rr, t = on_chip(cg_first_kernel, "cg_first", [parts, vec, small, row],
-                                  x, g2, scale, w, curv, scratch=tmp)
+        if it == 0:
+            g2, z_got = lax.optimization_barrier((reduce_permutes(gpart), z_got))
+        else:
+            g2 = reduce_rest(gpart)
+        if it == 0:
+            x, hpart, p, rr, t = pl.pallas_call(
+                cg_load_kernel,
+                in_specs=[hbm] + [vmem] * 4,
+                out_specs=[vmem] * 5,
+                out_shape=[jax.ShapeDtypeStruct((rows, f), BF16)]
+                + [jax.ShapeDtypeStruct(*o) for o in (parts, vec, small, row)],
+                scratch_shapes=tmp + [pltpu.SemaphoreType.DMA((STEPS,))],
+                compiler_params=pltpu.CompilerParams(vmem_limit_bytes=STAGE_LIMIT),
+                name="cg_load",
+            )(pltpu.with_memory_space_constraint(features, pltpu.HBM), g2, scale, w, curv)
+        else:
+            hpart, p, rr, t = on_chip(cg_first_kernel, "cg_first", [parts, vec, small, row],
+                                      x, g2, scale, w, curv, scratch=tmp)
         h2 = reduce_rest(hpart)
-        if it == 0:
-            h2, z_got = lax.optimization_barrier((h2, z_got))
         hpart, p, r, u, rr, t, m = on_chip(
             cg_next_kernel, "cg_next", [parts, vec, vec, vec, small, row, row],
             x, h2, scale, curv, p, rr, t, scratch=tmp)
@@ -492,7 +550,8 @@
         scratch_shapes=[pltpu.VMEM((1, slots), F32)] * 3
         + [pltpu.VMEM((fr, slots), BF16)] * 3
         + [pltpu.VMEM((MEM_DEV * fr, 128), F32)] * 4
-        + [pltpu.VMEM((slots, fr), BF16), pltpu.SemaphoreType.DMA(())],
+        + [pltpu.VMEM((slots, fr), BF16), pltpu.VMEM((MEM_DEV, slots), F32),
+           pltpu.SemaphoreType.DMA(())],
         compiler_params=pltpu.CompilerParams(vmem_limit_bytes=VMEM_LIMIT),
         name="members",
     )(z_got, got, part, rr, w, u, p)

time: 312 us -> 300 us (0.962)
  blocking collectives: 253 us -> 188 us
  starting transfers between devices: 0 us -> 31.8 us
  waiting for transfers between devices: 0 us -> 15.3 us
  Pallas kernels: 57 us -> 63.6 us
    all_to_all x16 -> x14, blocking collectives: 222 us -> 188 us  [exchange(): return lax.all_to_all(v, axes, 0, 0, tiled=True)]
    all_to_all x1 -> x0, blocking collectives: 31.2 us -> none  [on_device(): lax.all_to_all(packed.reshape(n_mem, cap, fr), ('y', 'z'), 0, 0, tiled=True)]
    ppermute x0 -> x12, starting transfers between devices: none -> 19.8 us  [reduce_permutes(): moved = [lax.ppermute(v, axes, flip(index, size)) for index in maps]]
    ppermute x0 -> x12, waiting for transfers between devices: none -> 15.3 us  [reduce_permutes(): moved = [lax.ppermute(v, axes, flip(index, size)) for index in maps]]
    all_to_all x0 -> x1, starting transfers between devices: none -> 12 us  [on_device(): lax.all_to_all(packed.reshape(n_mem, cap, fr), ('y', 'z'), 0, 0, tiled=True)]
    pallas_call x0 -> x1, Pallas kernels: none -> 6.3 us  [on_device(): pl.pallas_call(cg_load_kernel, in_specs=[hbm] + [vmem] * 4, out_specs=[vm...]
    pallas_call x1, Pallas kernels: 20.9 us -> 25.6 us  [on_device(): pl.pallas_call(member_kernel, in_specs=[pl.BlockSpec(memory_space=pltpu.H...]
    pallas_call x14 -> x16, Pallas kernels: 27.4 us -> 23 us  [on_chip(): pl.pallas_call(kernel, in_specs=[vmem] * len(ins), out_specs=[vmem] * len...]
  transfers between devices with their start and end apart: 0 -> 13, of which waited for: 0 -> 8; matrix products, arithmetic and copies ran while one was open for 0% -> 0% of each run, Pallas kernels for 0% -> 0%
where the time goes in v1:
time: 300 us
  blocking collectives  188 us (63%)
  Pallas kernels  63.6 us (21%)
  starting transfers between devices  31.8 us (11%)
  waiting for transfers between devices  15.3 us (5%)
    all_to_all x14, blocking collectives, exchange(): return lax.all_to_all(v, axes, 0, 0, tiled=True)  188 us
    pallas_call x1, Pallas kernels, on_device(): pl.pallas_call(member_kernel, in_specs=[pl.BlockSpec(memory_space=pltpu.H...  25.6 us
    pallas_call x16, Pallas kernels, on_chip(): pl.pallas_call(kernel, in_specs=[vmem] * len(ins), out_specs=[vmem] * len...  23 us
    ppermute x12, starting transfers between devices, reduce_permutes(): moved = [lax.ppermute(v, axes, flip(index, size)) for index in maps]  19.8 us
    ppermute x12, waiting for transfers between devices, reduce_permutes(): moved = [lax.ppermute(v, axes, flip(index, size)) for index in maps]  15.3 us
    all_to_all x1, starting transfers between devices, on_device(): lax.all_to_all(packed.reshape(n_mem, cap, fr), ('y', 'z'), 0, 0, tiled=True)  12 us
    pallas_call x1, Pallas kernels, on_device(): pl.pallas_call(start_kernel, in_specs=[hbm] * 8, out_specs=[hbm] + [vmem]...  7.67 us
    pallas_call x1, Pallas kernels, on_device(): pl.pallas_call(cg_load_kernel, in_specs=[hbm] + [vmem] * 4, out_specs=[vm...  6.3 us
  transfers between devices with their start and end apart: 13, of which 8 were waited for; matrix products, arithmetic and copies ran while one was open for 0% of the time, Pallas kernels for 0%

profile of v1, /device:TPU:1, one launch (start us, length us, event | category | flops | bytes accessed | tf_op | source)
XLA Modules:
  0.0 299.8 jit_solution(8731905616096689633)
XLA Ops:
  0.6 7.7 %start.1 = (bf16[2048,256]{1,0:T(8,128)(2,1)}, s32[1,1024]{1,0:T(1,128)S(1)}, f32[1,1024]{1,0:T(1,128)S(1)}, f32[1,1024]{1,0:T(1,128)S(1)}, f32[1,1024]{1,0:T(1,...) custom-call(bf16[1024,4096]{1,0:T(8,128)(2,1)} %x_hbm.3, ...), custom_call_target="tpu_custom_call" | custom-call | tf_op jit(solution)/shard_map/start/pallas_call | solution.py:485
  8.3 12.0 %all-to-all-start = ((bf16[32,64,256]{2,1,0:T(8,128)(2,1)}), bf16[32,64,256]{2,1,0:T(8,128)(2,1)S(1)}, u32[]{:S(2)}, u32[]{:S(2)}) async-start(bf16[32,64,256]{2,1,0:T(8,128)(2,1)} %bitcast.11), calls=%async_computation | async-start | bytes 2097152 | tf_op jit(solution)/shard_map/all_to_all | solution.py:500
  34.0 9.0 %collective-permute-start.8 = (f32[1,1,4096]{2,1,0:T(1,128)S(1)}, f32[1,1,4096]{2,1,0:T(1,128)S(1)}, u32[]{:S(2)}, u32[]{:S(2)}) collective-permute-start(f32[1,1,4096]{2,1,0:T(1,128)S(1)} %add_four.5.a_ref), channel_id=1, source_target_pairs={{0,36},{1,37},{2,38},{3,39},{4,32},{5,33},{6,34},{7,35},{32,4},{33... | collective-permute-start | bytes 49160 | tf_op jit(solution)/shard_map/ppermute | solution.py:472
  43.5 6.1 %collective-permute-done.8.d_ref = f32[1,1,4096]{2,1,0:T(1,128)S(1)} collective-permute-done((f32[1,1,4096]{2,1,0:T(1,128)S(1)}, f32[1,1,4096]{2,1,0:T(1,128)S(1)}, u32[]{:S(2)}, u32[]{:S(2)}) %collective-permute-start.8) | collective-permute-done | bytes 16416 | tf_op jit(solution)/shard_map/ppermute | solution.py:472
  55.5 6.3 %cg_load.1 = (bf16[1024,4096]{1,0:T(8,128)(2,1)S(1)}, f32[16,1,4096]{2,1,0:T(1,128)S(1)}, f32[1,4096]{1,0:T(1,128)S(1)}, f32[1,128]{1,0:T(1,128)S(1)}, f32[1,1024]{1,0:T(1,128)S(1)}) custom-call(bf16[1024,4096]{1,0:T(8,128)(2,1)} %x_hbm.3, f32[1,1,4096]{2,1,0:T(1,128)S(1)} %add_four.7.sum_ref, f32[1,4096]{1,0:T(1,128)S(1)} %get-tuple-element.59.scale_ref, ...), custom_call_target="tpu_custom_call" | custom-call | tf_op jit(solution)/shard_map/cg_load/pallas_call | solution.py:508
  61.8 14.4 %all_to_all.75.sum_ref = f32[16,1,4096]{2,1,0:T(1,128)S(1)} all-to-all(f32[16,1,4096]{2,1,0:T(1,128)S(1)} %get-tuple-element.63), channel_id=1, replica_groups=mesh['x'=4,'core'=2,'y'=4,'z'=8] {'core','z'}, dimensions={0} | all-to-all | bytes 524288 | tf_op jit(solution)/shard_map/all_to_all | solution.py:453
  76.2 13.3 %all_to_all.76.sum_ref = f32[16,1,4096]{2,1,0:T(1,128)S(1)} all-to-all(f32[16,1,4096]{2,1,0:T(1,128)S(1)} %again.5), channel_id=1, replica_groups=mesh['x'=4,'core'=2,'y'=4,'z'=8] {'x','y'}, dimensions={0} | all-to-all | bytes 524288 | tf_op jit(solution)/shard_map/all_to_all | solution.py:453
  89.5 4.7 %cg_next.2 = (f32[16,1,4096]{2,1,0:T(1,128)S(1)}, f32[1,4096]{1,0:T(1,128)S(1)}, f32[1,4096]{1,0:T(1,128)S(1)}, f32[1,4096]{1,0:T(1,128)S(1)}, f32[1,128]{1,0:T(...) custom-call(bf16[1024,4096]{1,0:T(8,128)(2,1)S(1)} %get-tuple-element.62.x_ref, ...), custom_call_target="tpu_custom_call" | custom-call | tf_op jit(solution)/shard_map/cg_next/pallas_call | solution.py:427
  94.3 16.0 %all_to_all.77.sum_ref = f32[16,1,4096]{2,1,0:T(1,128)S(1)} all-to-all(f32[16,1,4096]{2,1,0:T(1,128)S(1)} %get-tuple-element.67), channel_id=1, replica_groups=mesh['x'=4,'core'=2,'y'=4,'z'=8] {'core','z'}, dimensions={0} | all-to-all | bytes 524288 | tf_op jit(solution)/shard_map/all_to_all | solution.py:453
  110.3 10.5 %all_to_all.78.sum_ref = f32[16,1,4096]{2,1,0:T(1,128)S(1)} all-to-all(f32[16,1,4096]{2,1,0:T(1,128)S(1)} %again.6), channel_id=1, replica_groups=mesh['x'=4,'core'=2,'y'=4,'z'=8] {'x','y'}, dimensions={0} | all-to-all | bytes 524288 | tf_op jit(solution)/shard_map/all_to_all | solution.py:453
  124.1 22.0 %all_to_all.79.part_ref = f32[256,1,128]{2,1,0:T(1,128)S(1)} all-to-all(f32[256,1,128]{2,1,0:T(1,128)S(1)} %get-tuple-element.74), channel_id=1, replica_groups=mesh['x'=4,'core'=2,'y'=4,'z'=8] {'x','core','y','z'}, dimensions={0} | all-to-all | bytes 262144 | tf_op jit(solution)/shard_map/all_to_all | solution.py:453
  147.9 12.4 %all_to_all.80.sum_ref = f32[16,1,4096]{2,1,0:T(1,128)S(1)} all-to-all(f32[16,1,4096]{2,1,0:T(1,128)S(1)} %get-tuple-element.83), channel_id=1, replica_groups=mesh['x'=4,'core'=2,'y'=4,'z'=8] {'core','z'}, dimensions={0} | all-to-all | bytes 524288 | tf_op jit(solution)/shard_map/all_to_all | solution.py:453
  160.3 10.3 %all_to_all.81.sum_ref = f32[16,1,4096]{2,1,0:T(1,128)S(1)} all-to-all(f32[16,1,4096]{2,1,0:T(1,128)S(1)} %again.7), channel_id=1, replica_groups=mesh['x'=4,'core'=2,'y'=4,'z'=8] {'x','y'}, dimensions={0} | all-to-all | bytes 524288 | tf_op jit(solution)/shard_map/all_to_all | solution.py:453
  170.6 4.4 %cg_first.1 = (f32[16,1,4096]{2,1,0:T(1,128)S(1)}, f32[1,4096]{1,0:T(1,128)S(1)}, f32[1,128]{1,0:T(1,128)S(1)}, f32[1,1024]{1,0:T(1,128)S(1)}) custom-call(bf16[1024,4096]{1,0:T(8,128)(2,1)S(1)} %get-tuple-element.62.x_ref, f32[16,1,4096]{2,1,0:T(1,128)S(1)} %all_to_all.81.sum_ref, f32[1,4096]{1,0:T(1,128)S(1)} %get-tuple-element.59.scale_ref, ...), custom_call_target="tpu_custom_call" | custom-call | tf_op jit(solution)/shard_map/cg_first/pallas_call | solution.py:427
  175.1 16.0 %all_to_all.82.sum_ref = f32[16,1,4096]{2,1,0:T(1,128)S(1)} all-to-all(f32[16,1,4096]{2,1,0:T(1,128)S(1)} %get-tuple-element.86), channel_id=1, replica_groups=mesh['x'=4,'core'=2,'y'=4,'z'=8] {'core','z'}, dimensions={0} | all-to-all | bytes 524288 | tf_op jit(solution)/shard_map/all_to_all | solution.py:453
  191.1 10.5 %all_to_all.83.sum_ref = f32[16,1,4096]{2,1,0:T(1,128)S(1)} all-to-all(f32[16,1,4096]{2,1,0:T(1,128)S(1)} %again.8), channel_id=1, replica_groups=mesh['x'=4,'core'=2,'y'=4,'z'=8] {'x','y'}, dimensions={0} | all-to-all | bytes 524288 | tf_op jit(solution)/shard_map/all_to_all | solution.py:453
  201.6 4.7 %cg_next.3 = (f32[16,1,4096]{2,1,0:T(1,128)S(1)}, f32[1,4096]{1,0:T(1,128)S(1)}, f32[1,4096]{1,0:T(1,128)S(1)}, f32[1,4096]{1,0:T(1,128)S(1)}, f32[1,128]{1,0:T(...) custom-call(bf16[1024,4096]{1,0:T(8,128)(2,1)S(1)} %get-tuple-element.62.x_ref, ...), custom_call_target="tpu_custom_call" | custom-call | tf_op jit(solution)/shard_map/cg_next/pallas_call | solution.py:427
  206.3 16.0 %all_to_all.84.sum_ref = f32[16,1,4096]{2,1,0:T(1,128)S(1)} all-to-all(f32[16,1,4096]{2,1,0:T(1,128)S(1)} %get-tuple-element.90), channel_id=1, replica_groups=mesh['x'=4,'core'=2,'y'=4,'z'=8] {'core','z'}, dimensions={0} | all-to-all | bytes 524288 | tf_op jit(solution)/shard_map/all_to_all | solution.py:453
  222.4 10.5 %all_to_all.85.sum_ref = f32[16,1,4096]{2,1,0:T(1,128)S(1)} all-to-all(f32[16,1,4096]{2,1,0:T(1,128)S(1)} %again.9), channel_id=1, replica_groups=mesh['x'=4,'core'=2,'y'=4,'z'=8] {'x','y'}, dimensions={0} | all-to-all | bytes 524288 | tf_op jit(solution)/shard_map/all_to_all | solution.py:453
  232.9 3.7 %cg_last_pack.1 = (f32[32,1,256]{2,1,0:T(1,128)S(1)}, f32[1,4096]{1,0:T(1,128)S(1)}, f32[1,4096]{1,0:T(1,128)S(1)}, f32[1,128]{1,0:T(1,128)S(1)}) custom-call(bf16[1024,4096]{1,0:T(8,128)(2,1)S(1)} %get-tuple-element.62.x_ref, f32[16,1,4096]{2,1,0:T(1,128)S(1)} %all_to_all.85.sum_ref, f32[1,4096]{1,0:T(1,128)S(1)} %get-tuple-element.59.scale_ref, ...), custom_call_target="tpu_custom_call" | custom-call | tf_op jit(solution)/shard_map/cg_last_pack/pallas_call | solution.py:427
  236.6 15.1 %all_to_all.86.arr_ref = f32[32,1,256]{2,1,0:T(1,128)S(1)} all-to-all(f32[32,1,256]{2,1,0:T(1,128)S(1)} %get-tuple-element.100), channel_id=1, replica_groups=mesh['x'=4,'core'=2,'y'=4,'z'=8] {'y','z'}, dimensions={0} | all-to-all | bytes 65536 | tf_op jit(solution)/shard_map/all_to_all | solution.py:453
  251.8 9.7 %all_to_all.87.part_ref = f32[8,1,128]{2,1,0:T(1,128)S(1)} all-to-all(f32[8,1,128]{2,1,0:T(1,128)S(1)} %part.1), channel_id=1, replica_groups=mesh['x'=4,'core'=2,'y'=4,'z'=8] {'x','core'}, dimensions={0} | all-to-all | bytes 8192 | tf_op jit(solution)/shard_map/all_to_all | solution.py:453
  261.5 25.6 %members.1 = (f32[1,4096]{1,0:T(1,128)}, f32[8,256]{1,0:T(8,128)}, f32[32,1,64]{2,1,0:T(1,128)S(1)}) custom-call(bf16[2048,256]{1,0:T(8,128)(2,1)} %bitcast.10, f32[32,1,256]{2,1,0:T(1,128)S(1)} %all_to_all.86.arr_ref, f32[8,1,128]{2,1,0:T(1,128)S(1)} %all_to_all.87.part_ref, f32[1,128]{1,0:T(1,128)S(1)} %get-tuple-element.101.rr_ref, ...), custom_call_target="tpu_custom_call" | custom-call | tf_op jit(solution)/shard_map/members/pallas_call | solution.py:544
  287.1 11.6 %all_to_all.88.back_ref = f32[32,1,64]{2,1,0:T(1,128)S(1)} all-to-all(f32[32,1,64]{2,1,0:T(1,128)S(1)} %get-tuple-element.106), channel_id=1, replica_groups=mesh['x'=4,'core'=2,'y'=4,'z'=8] {'y','z'}, dimensions={0} | all-to-all | bytes 16384 | tf_op jit(solution)/shard_map/all_to_all | solution.py:453
  (38 shorter events, 26.4 us)
Async XLA Ops:
  8.3 47.2 %all-to-all-start = ((bf16[32,64,256]{2,1,0:T(8,128)(2,1)}), bf16[32,64,256]{2,1,0:T(8,128)(2,1)S(1)}, u32[]{:S(2)}, u32[]{:S(2)}) async-start(bf16[32,64,256]{2,1,0:T(8,128)(2,1)} %bitcast.11), calls=%async_computation | async-start | bytes 2097152 | tf_op jit(solution)/shard_map/all_to_all | solution.py:500
  20.4 3.9 %collective-permute-start.2 = (f32[1,1,4096]{2,1,0:T(1,128)S(1)}, f32[1,1,4096]{2,1,0:T(1,128)S(1)}, u32[]{:S(2)}, u32[]{:S(2)}) collective-permute-start(f32[1,1,4096]{2,1,0:T(1,128)S(1)} %get-tuple-element.55.a_ref), channel_id=1, source_target_pairs={{0,192},{64,128},{128,64},{192,0},{1,193},{65,129},{129,65},{193,1... | collective-permute-start | bytes 49160 | tf_op jit(solution)/shard_map/ppermute | solution.py:472
  22.9 4.1 %collective-permute-start.1 = (f32[1,1,4096]{2,1,0:T(1,128)S(1)}, f32[1,1,4096]{2,1,0:T(1,128)S(1)}, u32[]{:S(2)}, u32[]{:S(2)}) collective-permute-start(f32[1,1,4096]{2,1,0:T(1,128)S(1)} %get-tuple-element.55.a_ref), channel_id=1, source_target_pairs={{0,128},{64,192},{128,0},{192,64},{1,129},{65,193},{129,1},{193,65... | collective-permute-start | bytes 49160 | tf_op jit(solution)/shard_map/ppermute | solution.py:472
  23.5 3.6 %collective-permute-start = (f32[1,1,4096]{2,1,0:T(1,128)S(1)}, f32[1,1,4096]{2,1,0:T(1,128)S(1)}, u32[]{:S(2)}, u32[]{:S(2)}) collective-permute-start(f32[1,1,4096]{2,1,0:T(1,128)S(1)} %get-tuple-element.55.a_ref), channel_id=1, source_target_pairs={{0,64},{64,0},{128,192},{192,128},{1,65},{65,1},{129,193},{193,129... | collective-permute-start | bytes 49160 | tf_op jit(solution)/shard_map/ppermute | solution.py:472
  27.0 4.4 %collective-permute-start.5 = (f32[1,1,4096]{2,1,0:T(1,128)S(1)}, f32[1,1,4096]{2,1,0:T(1,128)S(1)}, u32[]{:S(2)}, u32[]{:S(2)}) collective-permute-start(f32[1,1,4096]{2,1,0:T(1,128)S(1)} %add_four.4.a_ref), channel_id=1, source_target_pairs={{0,24},{8,16},{16,8},{24,0},{1,25},{9,17},{17,9},{25,1},{2,26},{10... | collective-permute-start | bytes 49160 | tf_op jit(solution)/shard_map/ppermute | solution.py:472
  29.6 4.4 %collective-permute-start.4 = (f32[1,1,4096]{2,1,0:T(1,128)S(1)}, f32[1,1,4096]{2,1,0:T(1,128)S(1)}, u32[]{:S(2)}, u32[]{:S(2)}) collective-permute-start(f32[1,1,4096]{2,1,0:T(1,128)S(1)} %add_four.4.a_ref), channel_id=1, source_target_pairs={{0,16},{8,24},{16,0},{24,8},{1,17},{9,25},{17,1},{25,9},{2,18},{10... | collective-permute-start | bytes 49160 | tf_op jit(solution)/shard_map/ppermute | solution.py:472
  30.2 3.8 %collective-permute-start.3 = (f32[1,1,4096]{2,1,0:T(1,128)S(1)}, f32[1,1,4096]{2,1,0:T(1,128)S(1)}, u32[]{:S(2)}, u32[]{:S(2)}) collective-permute-start(f32[1,1,4096]{2,1,0:T(1,128)S(1)} %add_four.4.a_ref), channel_id=1, source_target_pairs={{0,8},{8,0},{16,24},{24,16},{1,9},{9,1},{17,25},{25,17},{2,10},{10... | collective-permute-start | bytes 49160 | tf_op jit(solution)/shard_map/ppermute | solution.py:472
  34.0 15.6 %collective-permute-start.8 = (f32[1,1,4096]{2,1,0:T(1,128)S(1)}, f32[1,1,4096]{2,1,0:T(1,128)S(1)}, u32[]{:S(2)}, u32[]{:S(2)}) collective-permute-start(f32[1,1,4096]{2,1,0:T(1,128)S(1)} %add_four.5.a_ref), channel_id=1, source_target_pairs={{0,36},{1,37},{2,38},{3,39},{4,32},{5,33},{6,34},{7,35},{32,4},{33... | collective-permute-start | bytes 49160 | tf_op jit(solution)/shard_map/ppermute | solution.py:472
  43.0 7.4 %collective-permute-start.7 = (f32[1,1,4096]{2,1,0:T(1,128)S(1)}, f32[1,1,4096]{2,1,0:T(1,128)S(1)}, u32[]{:S(2)}, u32[]{:S(2)}) collective-permute-start(f32[1,1,4096]{2,1,0:T(1,128)S(1)} %add_four.5.a_ref), channel_id=1, source_target_pairs={{0,4},{1,5},{2,6},{3,7},{4,0},{5,1},{6,2},{7,3},{32,36},{33,37},{3... | collective-permute-start | bytes 49160 | tf_op jit(solution)/shard_map/ppermute | solution.py:472
  43.4 7.0 %collective-permute-start.6 = (f32[1,1,4096]{2,1,0:T(1,128)S(1)}, f32[1,1,4096]{2,1,0:T(1,128)S(1)}, u32[]{:S(2)}, u32[]{:S(2)}) collective-permute-start(f32[1,1,4096]{2,1,0:T(1,128)S(1)} %add_four.5.a_ref), channel_id=1, source_target_pairs={{0,32},{1,33},{2,34},{3,35},{4,36},{5,37},{6,38},{7,39},{32,0},{33... | collective-permute-start | bytes 49160 | tf_op jit(solution)/shard_map/ppermute | solution.py:472
  50.4 4.5 %collective-permute-start.11 = (f32[1,1,4096]{2,1,0:T(1,128)S(1)}, f32[1,1,4096]{2,1,0:T(1,128)S(1)}, u32[]{:S(2)}, u32[]{:S(2)}) collective-permute-start(f32[1,1,4096]{2,1,0:T(1,128)S(1)} %add_four.6.a_ref), channel_id=1, source_target_pairs={{0,3},{1,2},{2,1},{3,0},{4,7},{5,6},{6,5},{7,4},{8,11},{9,10},{10,... | collective-permute-start | bytes 49160 | tf_op jit(solution)/shard_map/ppermute | solution.py:472
  50.5 4.4 %collective-permute-start.10 = (f32[1,1,4096]{2,1,0:T(1,128)S(1)}, f32[1,1,4096]{2,1,0:T(1,128)S(1)}, u32[]{:S(2)}, u32[]{:S(2)}) collective-permute-start(f32[1,1,4096]{2,1,0:T(1,128)S(1)} %add_four.6.a_ref), channel_id=1, source_target_pairs={{0,2},{1,3},{2,0},{3,1},{4,6},{5,7},{6,4},{7,5},{8,10},{9,11},{10,... | collective-permute-start | bytes 49160 | tf_op jit(solution)/shard_map/ppermute | solution.py:472
  52.1 3.4 %collective-permute-start.9 = (f32[1,1,4096]{2,1,0:T(1,128)S(1)}, f32[1,1,4096]{2,1,0:T(1,128)S(1)}, u32[]{:S(2)}, u32[]{:S(2)}) collective-permute-start(f32[1,1,4096]{2,1,0:T(1,128)S(1)} %add_four.6.a_ref), channel_id=1, source_target_pairs={{0,1},{1,0},{2,3},{3,2},{4,5},{5,4},{6,7},{7,6},{8,9},{9,8},{10,11... | collective-permute-start | bytes 49160 | tf_op jit(solution)/shard_map/ppermute | solution.py:472
  55.5 38.8 %copy-start = (bf16[32,64,256]{2,1,0:T(8,128)(2,1)}, bf16[32,64,256]{2,1,0:T(8,128)(2,1)S(1)}, u32[]{:S(2)}) copy-start(bf16[32,64,256]{2,1,0:T(8,128)(2,1)S(1)} %all-to-all-done) | copy-start | bytes 3145732

commit v2 on v1

--- a/solution.py
+++ b/solution.py
@@ -12,8 +12,10 @@
 PANEL = 16
 BLOCK = 8
 STEPS = 4
-UNROLL = 4
-GRAM_UNROLL = 1
+F_STEPS = 4
+B_STEPS = 2
+UNROLL = 8
+GRAMS = 2
 F32 = jnp.float32
 BF16 = jnp.bfloat16
 HIGH = lax.Precision.HIGHEST
@@ -58,7 +60,8 @@
 
 def forward(xs, x_ref, xs_ref, row_ref, arrive=None):
     xs_ref[...] = xs
-    block = x_ref.shape[0] // STEPS
+    steps = F_STEPS if arrive is None else STEPS
+    block = x_ref.shape[0] // steps
 
     def body(i, carry):
         at = pl.multiple_of(i * block, block)
@@ -68,13 +71,13 @@
         row_ref[:, pl.ds(at, block)] = both[0:1] + both[1:2]
         return carry
 
-    lax.fori_loop(0, STEPS, body, 0)
+    lax.fori_loop(0, steps, body, 0)
     return row_ref[...]
 
 
 def backward(row, x_ref, split_ref, out_ref):
     split_ref[...] = split_rows(row)
-    block = x_ref.shape[1] // STEPS
+    block = x_ref.shape[1] // B_STEPS
 
     def body(i, carry):
         at = pl.multiple_of(i * block, block)
@@ -84,7 +87,7 @@
             out_ref[j, :, pl.ds(at, block)] = val
         return carry
 
-    lax.fori_loop(0, STEPS, body, 0)
+    lax.fori_loop(0, B_STEPS, body, 0)
 
 
 def start_kernel(x_hbm, z_hbm, slot_hbm, member_hbm, lab_hbm, off_hbm, scale_hbm, w_hbm,
@@ -107,14 +110,19 @@
     loads[0].wait()
     loads[1].wait()
     size = buf.shape[1]
-    stores = []
-    for b in range(buf.shape[0]):
+
+    def store(b):
+        at = b * size if isinstance(b, int) else pl.multiple_of(b * size, size)
+        return pltpu.make_async_copy(buf.at[b], packed_ref.at[pl.ds(at, size)], psems.at[b])
+
+    def pack(b, carry):
         rows = lax.broadcasted_iota(jnp.int32, (size, slot_ref.shape[1]), 0) + b * size
         hot = jnp.where(rows == slot_ref[...], 1.0, 0.0).astype(BF16)
         buf[b] = dot_nn(hot, z_ref[...]).astype(BF16)
-        stores.append(pltpu.make_async_copy(
-            buf.at[b], packed_ref.at[pl.ds(b * size, size)], psems.at[b]))
-        stores[-1].start()
+        store(b).start()
+        return carry
+
+    lax.fori_loop(0, buf.shape[0], pack, 0)
     for load in loads[2:]:
         load.wait()
     labels = int_ref[...]
@@ -125,8 +133,8 @@
     prob = sigmoid(score + off_ref[...])
     curv_ref[...] = prob * (1.0 - prob)
     backward(prob - lab_ref[...], x_ref, split_ref, out_ref)
-    for store in stores:
-        store.wait()
+    for b in range(buf.shape[0]):
+        store(b).wait()
 
 
 def grad_next_kernel(x_ref, part_ref, rr_ref, w_ref, u_ref, p_ref, score_ref, t_ref, m_ref,
@@ -232,8 +240,12 @@
         out_ref[i] = val
 
 
-def add_four_kernel(a_ref, b_ref, c_ref, d_ref, out_ref):
-    out_ref[...] = (a_ref[...] + b_ref[...]) + (c_ref[...] + d_ref[...])
+def add_kernel(*refs):
+    out_ref = refs[-1]
+    vals = [ref[...] for ref in refs[:-1]]
+    while len(vals) > 1:
+        vals = [vals[i] + vals[i + 1] for i in range(0, len(vals), 2)]
+    out_ref[...] = vals[0]
 
 
 def part_kernel(arr_ref, out_ref):
@@ -299,7 +311,8 @@
 
 def member_kernel(z_hbm, arr_ref, part_ref, rr_ref, w_ref, u_ref, p_ref,
                   w_out, coef_ref, back_ref,
-                  base, tvec, code, zt, hi, lo, mat0, mat1, red0, red1, z_ref, hot_ref, sem):
+                  base, tvec, code, zt, hi, lo, mat0, mat1, red0, red1, z_ref, hot_ref,
+                  left_ref, sem):
     copy = pltpu.make_async_copy(z_hbm, z_ref, sem)
     copy.start()
     owners = arr_ref.shape[0]
@@ -338,13 +351,19 @@
                     == lax.broadcasted_iota(jnp.int32, (fr, fr), 1), RIDGE, 0.0)
     hot_ref[...] = onehot
 
-    def one_gram(m, carry):
-        mask = hot_ref[pl.ds(m, 1), :].astype(BF16)
-        gram = dot_nn(hi[...] * mask, z_ref[...]) + dot_nn(lo[...] * mask, z_ref[...])
-        put_lanes(mat, pl.ds(pl.multiple_of(m * fr, fr), fr), 0, gram + eye)
+    def some_grams(step, carry):
+        for j in range(GRAMS):
+            mask = hot_ref[pl.ds(step * GRAMS + j, 1), :].astype(BF16)
+            left_ref[2 * j * fr:(2 * j + 1) * fr, :] = hi[...] * mask
+            left_ref[(2 * j + 1) * fr:(2 * j + 2) * fr, :] = lo[...] * mask
+        both = dot_nn(left_ref[...], z_ref[...])
+        for j in range(GRAMS):
+            gram = both[2 * j * fr:(2 * j + 1) * fr] + both[(2 * j + 1) * fr:(2 * j + 2) * fr]
+            at = pl.multiple_of((step * GRAMS + j) * fr, fr)
+            put_lanes(mat, pl.ds(at, fr), 0, gram + eye)
         return carry
 
-    lax.fori_loop(0, MEM_DEV, one_gram, 0, unroll=GRAM_UNROLL)
+    lax.fori_loop(0, MEM_DEV // GRAMS, some_grams, 0)
     rm = resid * onehot
     rm_high = rm.astype(BF16)
     rm_low = (rm - rm_high.astype(F32)).astype(BF16)
@@ -459,18 +478,11 @@
 
     def reduce_permutes(v):
         half = sizes["z"] // 2
-        def flip(index, size):
-            return [(i, index(i)) for i in range(size)]
-        nz = sizes["z"]
-        phases = [
-            ("x", sizes["x"], [lambda i, b=b: i ^ b for b in (1, 2, 3)]),
-            ("y", sizes["y"], [lambda i, b=b: i ^ b for b in (1, 2, 3)]),
-            (("core", "z"), n1, [lambda i, b=b: i ^ b for b in (nz, half, nz + half)]),
-            ("z", nz, [lambda i, b=b: i ^ b for b in (1, 2, 3)]),
-        ]
-        for axes, size, maps in phases:
-            moved = [lax.ppermute(v, axes, flip(index, size)) for index in maps]
-            v, = on_chip(add_four_kernel, "add_four", [((1, 1, f), F32)], v, *moved)
+        four = (1, 2, 3)
+        for axis, flips in (("x", four), ("core", (1,)), ("y", four), ("z", four), ("z", (half,))):
+            size = sizes[axis]
+            moved = [lax.ppermute(v, axis, [(i, i ^ b) for i in range(size)]) for b in flips]
+            v, = on_chip(add_kernel, "add", [((1, 1, f), F32)], v, *moved)
         return v
 
     tmp = [pltpu.VMEM((8, f), BF16), pltpu.VMEM((8, rows), BF16)]
@@ -551,6 +563,7 @@
         + [pltpu.VMEM((fr, slots), BF16)] * 3
         + [pltpu.VMEM((MEM_DEV * fr, 128), F32)] * 4
         + [pltpu.VMEM((slots, fr), BF16), pltpu.VMEM((MEM_DEV, slots), F32),
+           pltpu.VMEM((2 * GRAMS * fr, slots), BF16),
            pltpu.SemaphoreType.DMA(())],
         compiler_params=pltpu.CompilerParams(vmem_limit_bytes=VMEM_LIMIT),
         name="members",

time: 300 us -> 296 us (0.987)
  Pallas kernels: 63.6 us -> 58.7 us
  blocking collectives: 188 us -> 192 us
  starting transfers between devices: 31.8 us -> 28.4 us
    pallas_call x1, Pallas kernels: 25.6 us -> 21.9 us  [on_device(): pl.pallas_call(member_kernel, in_specs=[pl.BlockSpec(memory_space=pltpu.H...]
    ppermute x12 -> x11, starting transfers between devices: 19.8 us -> 16.3 us  [reduce_permutes(): lax.ppermute(v, axis, [(i, i ^ b) for i in range(size)])]
    all_to_all x14, blocking collectives: 188 us -> 192 us  [exchange(): return lax.all_to_all(v, axes, 0, 0, tiled=True)]
    pallas_call x16 -> x17, Pallas kernels: 23 us -> 22 us  [on_chip(): pl.pallas_call(kernel, in_specs=[vmem] * len(ins), out_specs=[vmem] * len...]
    ppermute x12 -> x11, waiting for transfers between devices: 15.3 us -> 15.9 us  [reduce_permutes(): lax.ppermute(v, axis, [(i, i ^ b) for i in range(size)])]
  transfers between devices with their start and end apart: 13 -> 12, of which waited for: 8 -> 8; matrix products, arithmetic and copies ran while one was open for 0% -> 0% of each run, Pallas kernels for 0% -> 0%
where the time goes in v2:
time: 296 us; the launch traced here: 295 us
  blocking collectives  192 us (65%)
  Pallas kernels  58.7 us (20%)
  starting transfers between devices  28.4 us (10%)
  waiting for transfers between devices  15.9 us (5%)
    all_to_all x14, blocking collectives, exchange(): return lax.all_to_all(v, axes, 0, 0, tiled=True)  192 us
    pallas_call x17, Pallas kernels, on_chip(): pl.pallas_call(kernel, in_specs=[vmem] * len(ins), out_specs=[vmem] * len...  22 us
    pallas_call x1, Pallas kernels, on_device(): pl.pallas_call(member_kernel, in_specs=[pl.BlockSpec(memory_space=pltpu.H...  21.9 us
    ppermute x11, starting transfers between devices, reduce_permutes(): lax.ppermute(v, axis, [(i, i ^ b) for i in range(size)])  16.3 us
    ppermute x11, waiting for transfers between devices, reduce_permutes(): lax.ppermute(v, axis, [(i, i ^ b) for i in range(size)])  15.9 us
    all_to_all x1, starting transfers between devices, on_device(): lax.all_to_all(packed.reshape(n_mem, cap, fr), ('y', 'z'), 0, 0, tiled=True)  12 us
    pallas_call x1, Pallas kernels, on_device(): pl.pallas_call(start_kernel, in_specs=[hbm] * 8, out_specs=[hbm] + [vmem]...  7.79 us
    pallas_call x1, Pallas kernels, on_device(): pl.pallas_call(cg_load_kernel, in_specs=[hbm] + [vmem] * 4, out_specs=[vm...  6.04 us
  transfers between devices with their start and end apart: 12, of which 8 were waited for; matrix products, arithmetic and copies ran while one was open for 0% of the time, Pallas kernels for 0%

profile of v2, /device:TPU:1, one launch (start us, length us, event | category | flops | bytes accessed | tf_op | source)
XLA Modules:
  0.0 295.4 jit_solution(14219050761918793909)
XLA Ops:
  0.6 7.8 %start.1 = (bf16[2048,256]{1,0:T(8,128)(2,1)}, s32[1,1024]{1,0:T(1,128)S(1)}, f32[1,1024]{1,0:T(1,128)S(1)}, f32[1,1024]{1,0:T(1,128)S(1)}, f32[1,1024]{1,0:T(1,...) custom-call(bf16[1024,4096]{1,0:T(8,128)(2,1)} %x_hbm.3, ...), custom_call_target="tpu_custom_call" | custom-call | tf_op jit(solution)/shard_map/start/pallas_call | solution.py:497
  8.4 12.0 %all-to-all-start = ((bf16[32,64,256]{2,1,0:T(8,128)(2,1)}), bf16[32,64,256]{2,1,0:T(8,128)(2,1)S(1)}, u32[]{:S(2)}, u32[]{:S(2)}) async-start(bf16[32,64,256]{2,1,0:T(8,128)(2,1)} %bitcast.11), calls=%async_computation | async-start | bytes 2097152 | tf_op jit(solution)/shard_map/all_to_all | solution.py:512
  34.7 3.3 %collective-permute-done.5.refs_2_ = f32[1,1,4096]{2,1,0:T(1,128)S(1)} collective-permute-done((f32[1,1,4096]{2,1,0:T(1,128)S(1)}, f32[1,1,4096]{2,1,0:T(1,128)S(1)}, u32[]{:S(2)}, u32[]{:S(2)}) %collective-permute-start.5) | collective-permute-done | bytes 16416 | tf_op jit(solution)/shard_map/ppermute | solution.py:484
  46.1 3.5 %collective-permute-start.10 = (f32[1,1,4096]{2,1,0:T(1,128)S(1)}, f32[1,1,4096]{2,1,0:T(1,128)S(1)}, u32[]{:S(2)}, u32[]{:S(2)}) collective-permute-start(f32[1,1,4096]{2,1,0:T(1,128)S(1)} %add.8.refs_0_), channel_id=1, source_target_pairs={{0,4},{1,5},{2,6},{3,7},{4,0},{5,1},{6,2},{7,3},{8,12},{9,13},{10,... | collective-permute-start | bytes 49160 | tf_op jit(solution)/shard_map/ppermute | solution.py:484
  52.7 6.0 %cg_load.1 = (bf16[1024,4096]{1,0:T(8,128)(2,1)S(1)}, f32[16,1,4096]{2,1,0:T(1,128)S(1)}, f32[1,4096]{1,0:T(1,128)S(1)}, f32[1,128]{1,0:T(1,128)S(1)}, f32[1,1024]{1,0:T(1,128)S(1)}) custom-call(bf16[1024,4096]{1,0:T(8,128)(2,1)} %x_hbm.3, f32[1,1,4096]{2,1,0:T(1,128)S(1)} %add.9.sum_ref, f32[1,4096]{1,0:T(1,128)S(1)} %get-tuple-element.59.scale_ref, ...), custom_call_target="tpu_custom_call" | custom-call | tf_op jit(solution)/shard_map/cg_load/pallas_call | solution.py:520
  58.8 17.1 %all_to_all.75.sum_ref = f32[16,1,4096]{2,1,0:T(1,128)S(1)} all-to-all(f32[16,1,4096]{2,1,0:T(1,128)S(1)} %get-tuple-element.63), channel_id=1, replica_groups=mesh['x'=4,'core'=2,'y'=4,'z'=8] {'core','z'}, dimensions={0} | all-to-all | bytes 524288 | tf_op jit(solution)/shard_map/all_to_all | solution.py:472
  75.9 13.9 %all_to_all.76.sum_ref = f32[16,1,4096]{2,1,0:T(1,128)S(1)} all-to-all(f32[16,1,4096]{2,1,0:T(1,128)S(1)} %again.5), channel_id=1, replica_groups=mesh['x'=4,'core'=2,'y'=4,'z'=8] {'x','y'}, dimensions={0} | all-to-all | bytes 524288 | tf_op jit(solution)/shard_map/all_to_all | solution.py:472
  89.8 4.5 %cg_next.2 = (f32[16,1,4096]{2,1,0:T(1,128)S(1)}, f32[1,4096]{1,0:T(1,128)S(1)}, f32[1,4096]{1,0:T(1,128)S(1)}, f32[1,4096]{1,0:T(1,128)S(1)}, f32[1,128]{1,0:T(...) custom-call(bf16[1024,4096]{1,0:T(8,128)(2,1)S(1)} %get-tuple-element.62.x_ref, ...), custom_call_target="tpu_custom_call" | custom-call | tf_op jit(solution)/shard_map/cg_next/pallas_call | solution.py:446
  94.3 16.0 %all_to_all.77.sum_ref = f32[16,1,4096]{2,1,0:T(1,128)S(1)} all-to-all(f32[16,1,4096]{2,1,0:T(1,128)S(1)} %get-tuple-element.67), channel_id=1, replica_groups=mesh['x'=4,'core'=2,'y'=4,'z'=8] {'core','z'}, dimensions={0} | all-to-all | bytes 524288 | tf_op jit(solution)/shard_map/all_to_all | solution.py:472
  110.4 10.5 %all_to_all.78.sum_ref = f32[16,1,4096]{2,1,0:T(1,128)S(1)} all-to-all(f32[16,1,4096]{2,1,0:T(1,128)S(1)} %again.6), channel_id=1, replica_groups=mesh['x'=4,'core'=2,'y'=4,'z'=8] {'x','y'}, dimensions={0} | all-to-all | bytes 524288 | tf_op jit(solution)/shard_map/all_to_all | solution.py:472
  124.2 22.0 %all_to_all.79.part_ref = f32[256,1,128]{2,1,0:T(1,128)S(1)} all-to-all(f32[256,1,128]{2,1,0:T(1,128)S(1)} %get-tuple-element.74), channel_id=1, replica_groups=mesh['x'=4,'core'=2,'y'=4,'z'=8] {'x','core','y','z'}, dimensions={0} | all-to-all | bytes 262144 | tf_op jit(solution)/shard_map/all_to_all | solution.py:472
  147.7 12.4 %all_to_all.80.sum_ref = f32[16,1,4096]{2,1,0:T(1,128)S(1)} all-to-all(f32[16,1,4096]{2,1,0:T(1,128)S(1)} %get-tuple-element.83), channel_id=1, replica_groups=mesh['x'=4,'core'=2,'y'=4,'z'=8] {'core','z'}, dimensions={0} | all-to-all | bytes 524288 | tf_op jit(solution)/shard_map/all_to_all | solution.py:472
  160.1 10.3 %all_to_all.81.sum_ref = f32[16,1,4096]{2,1,0:T(1,128)S(1)} all-to-all(f32[16,1,4096]{2,1,0:T(1,128)S(1)} %again.7), channel_id=1, replica_groups=mesh['x'=4,'core'=2,'y'=4,'z'=8] {'x','y'}, dimensions={0} | all-to-all | bytes 524288 | tf_op jit(solution)/shard_map/all_to_all | solution.py:472
  170.5 4.2 %cg_first.1 = (f32[16,1,4096]{2,1,0:T(1,128)S(1)}, f32[1,4096]{1,0:T(1,128)S(1)}, f32[1,128]{1,0:T(1,128)S(1)}, f32[1,1024]{1,0:T(1,128)S(1)}) custom-call(bf16[1024,4096]{1,0:T(8,128)(2,1)S(1)} %get-tuple-element.62.x_ref, f32[16,1,4096]{2,1,0:T(1,128)S(1)} %all_to_all.81.sum_ref, f32[1,4096]{1,0:T(1,128)S(1)} %get-tuple-element.59.scale_ref, ...), custom_call_target="tpu_custom_call" | custom-call | tf_op jit(solution)/shard_map/cg_first/pallas_call | solution.py:446
  174.6 16.0 %all_to_all.82.sum_ref = f32[16,1,4096]{2,1,0:T(1,128)S(1)} all-to-all(f32[16,1,4096]{2,1,0:T(1,128)S(1)} %get-tuple-element.86), channel_id=1, replica_groups=mesh['x'=4,'core'=2,'y'=4,'z'=8] {'core','z'}, dimensions={0} | all-to-all | bytes 524288 | tf_op jit(solution)/shard_map/all_to_all | solution.py:472
  190.7 10.5 %all_to_all.83.sum_ref = f32[16,1,4096]{2,1,0:T(1,128)S(1)} all-to-all(f32[16,1,4096]{2,1,0:T(1,128)S(1)} %again.8), channel_id=1, replica_groups=mesh['x'=4,'core'=2,'y'=4,'z'=8] {'x','y'}, dimensions={0} | all-to-all | bytes 524288 | tf_op jit(solution)/shard_map/all_to_all | solution.py:472
  201.2 4.5 %cg_next.3 = (f32[16,1,4096]{2,1,0:T(1,128)S(1)}, f32[1,4096]{1,0:T(1,128)S(1)}, f32[1,4096]{1,0:T(1,128)S(1)}, f32[1,4096]{1,0:T(1,128)S(1)}, f32[1,128]{1,0:T(...) custom-call(bf16[1024,4096]{1,0:T(8,128)(2,1)S(1)} %get-tuple-element.62.x_ref, ...), custom_call_target="tpu_custom_call" | custom-call | tf_op jit(solution)/shard_map/cg_next/pallas_call | solution.py:446
  205.7 16.0 %all_to_all.84.sum_ref = f32[16,1,4096]{2,1,0:T(1,128)S(1)} all-to-all(f32[16,1,4096]{2,1,0:T(1,128)S(1)} %get-tuple-element.90), channel_id=1, replica_groups=mesh['x'=4,'core'=2,'y'=4,'z'=8] {'core','z'}, dimensions={0} | all-to-all | bytes 524288 | tf_op jit(solution)/shard_map/all_to_all | solution.py:472
  221.7 10.5 %all_to_all.85.sum_ref = f32[16,1,4096]{2,1,0:T(1,128)S(1)} all-to-all(f32[16,1,4096]{2,1,0:T(1,128)S(1)} %again.9), channel_id=1, replica_groups=mesh['x'=4,'core'=2,'y'=4,'z'=8] {'x','y'}, dimensions={0} | all-to-all | bytes 524288 | tf_op jit(solution)/shard_map/all_to_all | solution.py:472
  232.2 3.7 %cg_last_pack.1 = (f32[32,1,256]{2,1,0:T(1,128)S(1)}, f32[1,4096]{1,0:T(1,128)S(1)}, f32[1,4096]{1,0:T(1,128)S(1)}, f32[1,128]{1,0:T(1,128)S(1)}) custom-call(bf16[1024,4096]{1,0:T(8,128)(2,1)S(1)} %get-tuple-element.62.x_ref, f32[16,1,4096]{2,1,0:T(1,128)S(1)} %all_to_all.85.sum_ref, f32[1,4096]{1,0:T(1,128)S(1)} %get-tuple-element.59.scale_ref, ...), custom_call_target="tpu_custom_call" | custom-call | tf_op jit(solution)/shard_map/cg_last_pack/pallas_call | solution.py:446
  235.9 15.1 %all_to_all.86.arr_ref = f32[32,1,256]{2,1,0:T(1,128)S(1)} all-to-all(f32[32,1,256]{2,1,0:T(1,128)S(1)} %get-tuple-element.100), channel_id=1, replica_groups=mesh['x'=4,'core'=2,'y'=4,'z'=8] {'y','z'}, dimensions={0} | all-to-all | bytes 65536 | tf_op jit(solution)/shard_map/all_to_all | solution.py:472
  251.1 9.7 %all_to_all.87.part_ref = f32[8,1,128]{2,1,0:T(1,128)S(1)} all-to-all(f32[8,1,128]{2,1,0:T(1,128)S(1)} %part.1), channel_id=1, replica_groups=mesh['x'=4,'core'=2,'y'=4,'z'=8] {'x','core'}, dimensions={0} | all-to-all | bytes 8192 | tf_op jit(solution)/shard_map/all_to_all | solution.py:472
  260.8 21.9 %members.1 = (f32[1,4096]{1,0:T(1,128)}, f32[8,256]{1,0:T(8,128)}, f32[32,1,64]{2,1,0:T(1,128)S(1)}) custom-call(bf16[2048,256]{1,0:T(8,128)(2,1)} %bitcast.10, f32[32,1,256]{2,1,0:T(1,128)S(1)} %all_to_all.86.arr_ref, f32[8,1,128]{2,1,0:T(1,128)S(1)} %all_to_all.87.part_ref, f32[1,128]{1,0:T(1,128)S(1)} %get-tuple-element.101.rr_ref, ...), custom_call_target="tpu_custom_call" | custom-call | tf_op jit(solution)/shard_map/members/pallas_call | solution.py:556
  282.7 11.6 %all_to_all.88.back_ref = f32[32,1,64]{2,1,0:T(1,128)S(1)} all-to-all(f32[32,1,64]{2,1,0:T(1,128)S(1)} %get-tuple-element.106), channel_id=1, replica_groups=mesh['x'=4,'core'=2,'y'=4,'z'=8] {'y','z'}, dimensions={0} | all-to-all | bytes 16384 | tf_op jit(solution)/shard_map/all_to_all | solution.py:472
  (37 shorter events, 31.6 us)
Async XLA Ops:
  8.4 44.3 %all-to-all-start = ((bf16[32,64,256]{2,1,0:T(8,128)(2,1)}), bf16[32,64,256]{2,1,0:T(8,128)(2,1)S(1)}, u32[]{:S(2)}, u32[]{:S(2)}) async-start(bf16[32,64,256]{2,1,0:T(8,128)(2,1)} %bitcast.11), calls=%async_computation | async-start | bytes 2097152 | tf_op jit(solution)/shard_map/all_to_all | solution.py:512
  20.5 3.9 %collective-permute-start.2 = (f32[1,1,4096]{2,1,0:T(1,128)S(1)}, f32[1,1,4096]{2,1,0:T(1,128)S(1)}, u32[]{:S(2)}, u32[]{:S(2)}) collective-permute-start(f32[1,1,4096]{2,1,0:T(1,128)S(1)} %get-tuple-element.55.refs_0_), channel_id=1, source_target_pairs={{0,192},{64,128},{128,64},{192,0},{1,193},{65,129},{129,65},{193,1... | collective-permute-start | bytes 49160 | tf_op jit(solution)/shard_map/ppermute | solution.py:484
  23.0 4.1 %collective-permute-start.1 = (f32[1,1,4096]{2,1,0:T(1,128)S(1)}, f32[1,1,4096]{2,1,0:T(1,128)S(1)}, u32[]{:S(2)}, u32[]{:S(2)}) collective-permute-start(f32[1,1,4096]{2,1,0:T(1,128)S(1)} %get-tuple-element.55.refs_0_), channel_id=1, source_target_pairs={{0,128},{64,192},{128,0},{192,64},{1,129},{65,193},{129,1},{193,65... | collective-permute-start | bytes 49160 | tf_op jit(solution)/shard_map/ppermute | solution.py:484
  23.6 3.6 %collective-permute-start = (f32[1,1,4096]{2,1,0:T(1,128)S(1)}, f32[1,1,4096]{2,1,0:T(1,128)S(1)}, u32[]{:S(2)}, u32[]{:S(2)}) collective-permute-start(f32[1,1,4096]{2,1,0:T(1,128)S(1)} %get-tuple-element.55.refs_0_), channel_id=1, source_target_pairs={{0,64},{64,0},{128,192},{192,128},{1,65},{65,1},{129,193},{193,129... | collective-permute-start | bytes 49160 | tf_op jit(solution)/shard_map/ppermute | solution.py:484
  27.2 3.3 %collective-permute-start.3 = (f32[1,1,4096]{2,1,0:T(1,128)S(1)}, f32[1,1,4096]{2,1,0:T(1,128)S(1)}, u32[]{:S(2)}, u32[]{:S(2)}) collective-permute-start(f32[1,1,4096]{2,1,0:T(1,128)S(1)} %add.5.refs_0_), channel_id=1, source_target_pairs={{0,32},{32,0},{1,33},{33,1},{2,34},{34,2},{3,35},{35,3},{4,36},{36... | collective-permute-start | bytes 49160 | tf_op jit(solution)/shard_map/ppermute | solution.py:484
  30.5 4.2 %collective-permute-start.6 = (f32[1,1,4096]{2,1,0:T(1,128)S(1)}, f32[1,1,4096]{2,1,0:T(1,128)S(1)}, u32[]{:S(2)}, u32[]{:S(2)}) collective-permute-start(f32[1,1,4096]{2,1,0:T(1,128)S(1)} %add.6.refs_0_), channel_id=1, source_target_pairs={{0,24},{8,16},{16,8},{24,0},{1,25},{9,17},{17,9},{25,1},{2,26},{10... | collective-permute-start | bytes 49160 | tf_op jit(solution)/shard_map/ppermute | solution.py:484
  33.2 4.7 %collective-permute-start.5 = (f32[1,1,4096]{2,1,0:T(1,128)S(1)}, f32[1,1,4096]{2,1,0:T(1,128)S(1)}, u32[]{:S(2)}, u32[]{:S(2)}) collective-permute-start(f32[1,1,4096]{2,1,0:T(1,128)S(1)} %add.6.refs_0_), channel_id=1, source_target_pairs={{0,16},{8,24},{16,0},{24,8},{1,17},{9,25},{17,1},{25,9},{2,18},{10... | collective-permute-start | bytes 49160 | tf_op jit(solution)/shard_map/ppermute | solution.py:484
  33.8 4.2 %collective-permute-start.4 = (f32[1,1,4096]{2,1,0:T(1,128)S(1)}, f32[1,1,4096]{2,1,0:T(1,128)S(1)}, u32[]{:S(2)}, u32[]{:S(2)}) collective-permute-start(f32[1,1,4096]{2,1,0:T(1,128)S(1)} %add.6.refs_0_), channel_id=1, source_target_pairs={{0,8},{8,0},{16,24},{24,16},{1,9},{9,1},{17,25},{25,17},{2,10},{10... | collective-permute-start | bytes 49160 | tf_op jit(solution)/shard_map/ppermute | solution.py:484
  38.0 5.1 %collective-permute-start.9 = (f32[1,1,4096]{2,1,0:T(1,128)S(1)}, f32[1,1,4096]{2,1,0:T(1,128)S(1)}, u32[]{:S(2)}, u32[]{:S(2)}) collective-permute-start(f32[1,1,4096]{2,1,0:T(1,128)S(1)} %add.7.refs_0_), channel_id=1, source_target_pairs={{0,3},{1,2},{2,1},{3,0},{4,7},{5,6},{6,5},{7,4},{8,11},{9,10},{10,... | collective-permute-start | bytes 49160 | tf_op jit(solution)/shard_map/ppermute | solution.py:484
  40.9 5.2 %collective-permute-start.8 = (f32[1,1,4096]{2,1,0:T(1,128)S(1)}, f32[1,1,4096]{2,1,0:T(1,128)S(1)}, u32[]{:S(2)}, u32[]{:S(2)}) collective-permute-start(f32[1,1,4096]{2,1,0:T(1,128)S(1)} %add.7.refs_0_), channel_id=1, source_target_pairs={{0,2},{1,3},{2,0},{3,1},{4,6},{5,7},{6,4},{7,5},{8,10},{9,11},{10,... | collective-permute-start | bytes 49160 | tf_op jit(solution)/shard_map/ppermute | solution.py:484
  40.9 5.2 %collective-permute-start.7 = (f32[1,1,4096]{2,1,0:T(1,128)S(1)}, f32[1,1,4096]{2,1,0:T(1,128)S(1)}, u32[]{:S(2)}, u32[]{:S(2)}) collective-permute-start(f32[1,1,4096]{2,1,0:T(1,128)S(1)} %add.7.refs_0_), channel_id=1, source_target_pairs={{0,1},{1,0},{2,3},{3,2},{4,5},{5,4},{6,7},{7,6},{8,9},{9,8},{10,11... | collective-permute-start | bytes 49160 | tf_op jit(solution)/shard_map/ppermute | solution.py:484
  46.1 6.6 %collective-permute-start.10 = (f32[1,1,4096]{2,1,0:T(1,128)S(1)}, f32[1,1,4096]{2,1,0:T(1,128)S(1)}, u32[]{:S(2)}, u32[]{:S(2)}) collective-permute-start(f32[1,1,4096]{2,1,0:T(1,128)S(1)} %add.8.refs_0_), channel_id=1, source_target_pairs={{0,4},{1,5},{2,6},{3,7},{4,0},{5,1},{6,2},{7,3},{8,12},{9,13},{10,... | collective-permute-start | bytes 49160 | tf_op jit(solution)/shard_map/ppermute | solution.py:484
  52.7 41.6 %copy-start = (bf16[32,64,256]{2,1,0:T(8,128)(2,1)}, bf16[32,64,256]{2,1,0:T(8,128)(2,1)S(1)}, u32[]{:S(2)}) copy-start(bf16[32,64,256]{2,1,0:T(8,128)(2,1)S(1)} %all-to-all-done) | copy-start | bytes 3145732

commit v3 on v2

--- a/solution.py
+++ b/solution.py
@@ -12,9 +12,8 @@
 PANEL = 16
 BLOCK = 8
 STEPS = 4
-F_STEPS = 4
+F_STEPS = 2
 B_STEPS = 2
-UNROLL = 8
 GRAMS = 2
 F32 = jnp.float32
 BF16 = jnp.bfloat16
@@ -58,9 +57,8 @@
     return acc
 
 
-def forward(xs, x_ref, xs_ref, row_ref, arrive=None):
+def forward(xs, x_ref, xs_ref, row_ref, arrive=None, steps=STEPS):
     xs_ref[...] = xs
-    steps = F_STEPS if arrive is None else STEPS
     block = x_ref.shape[0] // steps
 
     def body(i, carry):
@@ -159,7 +157,8 @@
     r = -(scale_ref[...] * sum_parts(sum_ref) + RIDGE * w_ref[...])
     p_out[...] = r
     rr_out[...] = jnp.broadcast_to(total(r * r), rr_out.shape)
-    t = forward(split_rows(scale_ref[...] * r), x_ref, xs_ref, t_ref, arrive)
+    t = forward(split_rows(scale_ref[...] * r), x_ref, xs_ref, t_ref, arrive,
+                STEPS if arrive else F_STEPS)
     backward(curv_ref[...] * t, x_ref, split_ref, out_ref)
 
 
@@ -197,7 +196,7 @@
                    out_ref, p_out, r_out, u_out, rr_out, t_ref, m_ref, xs_ref, split_ref):
     a, xs = cg_update(sum_ref, scale_ref, p_ref, p_ref, None, rr_ref, p_out, r_out, u_out, rr_out)
     m_ref[...] = a * t_in[...]
-    t = forward(xs, x_ref, xs_ref, t_ref)
+    t = forward(xs, x_ref, xs_ref, t_ref, steps=F_STEPS)
     backward(curv_ref[...] * t, x_ref, split_ref, out_ref)
 
 
@@ -369,9 +368,14 @@
     rm_low = (rm - rm_high.astype(F32)).astype(BF16)
     rhs = dot_nn(rm_high, z_ref[...]) + dot_nn(rm_low, z_ref[...])
 
+    def panel_rows(k0):
+        return [get_lanes(mat, pl.ds(k0 + i, MEM_DEV, stride=fr), (k0 // 128) * 128)
+                for i in range(PANEL)]
+
+    ahead = panel_rows(0)
     for k0 in range(0, fr, PANEL):
         lane0 = (k0 // 128) * 128
-        orig = [get_lanes(mat, pl.ds(k0 + i, MEM_DEV, stride=fr), lane0) for i in range(PANEL)]
+        orig = ahead
         wide = (MEM_DEV, 128)
         rows = [[o[:, c:c + 128] for c in range(0, o.shape[1], 128)]
                 + [jnp.broadcast_to(rhs[:, k0 + i:k0 + i + 1], wide)]
@@ -395,19 +399,27 @@
         if top < fr:
             lane1 = (top // 128) * 128
             row1 = lane1
-            def trailing(m, carry, k0=k0, row1=row1, lane1=lane1):
-                first = pl.multiple_of(m * fr, fr)
-                o = get_lanes(mat, pl.ds(first + k0, PANEL), row1)
+            lefts, rights = [], []
+            for m in range(MEM_DEV):
+                o = get_lanes(mat, pl.ds(m * fr + k0, PANEL), row1)
                 w = get_lanes(red, pl.ds(k0 * MEM_DEV + m, PANEL, stride=MEM_DEV), lane1)
                 o1, o2, o3 = three_parts(o)
                 w1, w2, w3 = three_parts(w)
                 left = jnp.concatenate([o1, o1, o2, o2, o1, o3], axis=0)
-                right = jnp.concatenate([w1, w2, w1, w2, w3, w1], axis=0)
-                rest = pl.ds(first + row1, fr - row1)
-                put_lanes(mat, rest, lane1, get_lanes(mat, rest, lane1) - dot_tn(left, right))
-                return carry
-
-            lax.fori_loop(0, MEM_DEV, trailing, 0, unroll=UNROLL)
+                lefts.append(left.T[top - row1:])
+                rights.append(jnp.concatenate([w1, w2, w1, w2, w3, w1], axis=0))
+
+            def trailing(m, skip, count):
+                rest = pl.ds(m * fr + top + skip, count)
+                put_lanes(mat, rest, lane1, get_lanes(mat, rest, lane1)
+                          - dot_nn(lefts[m][skip:skip + count], rights[m]))
+
+            for m in range(MEM_DEV):
+                trailing(m, 0, PANEL)
+            ahead = panel_rows(top)
+            if top + PANEL < fr:
+                for m in range(MEM_DEV):
+                    trailing(m, PANEL, fr - top - PANEL)
 
     lanes = lax.broadcasted_iota(jnp.int32, rhs.shape, 1)
     sol = jnp.where(lanes >= fr - PANEL, rhs, 0.0)

time: 296 us -> 294 us (level)
  no operation moved by 1% of the time
where the time goes in v3:
time: 294 us; the launch traced here: 293 us
  blocking collectives  192 us (65%)
  Pallas kernels  56.4 us (19%)
  starting transfers between devices  28.4 us (10%)
  waiting for transfers between devices  15.9 us (5%)
    all_to_all x14, blocking collectives, exchange(): return lax.all_to_all(v, axes, 0, 0, tiled=True)  192 us
    pallas_call x17, Pallas kernels, on_chip(): pl.pallas_call(kernel, in_specs=[vmem] * len(ins), out_specs=[vmem] * len...  21.2 us
    pallas_call x1, Pallas kernels, on_device(): pl.pallas_call(member_kernel, in_specs=[pl.BlockSpec(memory_space=pltpu.H...  20.4 us
    ppermute x11, starting transfers between devices, reduce_permutes(): lax.ppermute(v, axis, [(i, i ^ b) for i in range(size)])  16.3 us
    ppermute x11, waiting for transfers between devices, reduce_permutes(): lax.ppermute(v, axis, [(i, i ^ b) for i in range(size)])  15.9 us
    all_to_all x1, starting transfers between devices, on_device(): lax.all_to_all(packed.reshape(n_mem, cap, fr), ('y', 'z'), 0, 0, tiled=True)  12 us
    pallas_call x1, Pallas kernels, on_device(): pl.pallas_call(start_kernel, in_specs=[hbm] * 8, out_specs=[hbm] + [vmem]...  7.79 us
    pallas_call x1, Pallas kernels, on_device(): pl.pallas_call(cg_load_kernel, in_specs=[hbm] + [vmem] * 4, out_specs=[vm...  6.04 us
  transfers between devices with their start and end apart: 12, of which 8 were waited for; matrix products, arithmetic and copies ran while one was open for 0% of the time, Pallas kernels for 0%

profile of v3, /device:TPU:1, one launch (start us, length us, event | category | flops | bytes accessed | tf_op | source)
XLA Modules:
  0.0 293.1 jit_solution(12699869480983709096)
XLA Ops:
  0.6 7.8 %start.1 = (bf16[2048,256]{1,0:T(8,128)(2,1)}, s32[1,1024]{1,0:T(1,128)S(1)}, f32[1,1024]{1,0:T(1,128)S(1)}, f32[1,1024]{1,0:T(1,128)S(1)}, f32[1,1024]{1,0:T(1,...) custom-call(bf16[1024,4096]{1,0:T(8,128)(2,1)} %x_hbm.3, ...), custom_call_target="tpu_custom_call" | custom-call | tf_op jit(solution)/shard_map/start/pallas_call | solution.py:509
  8.4 12.0 %all-to-all-start = ((bf16[32,64,256]{2,1,0:T(8,128)(2,1)}), bf16[32,64,256]{2,1,0:T(8,128)(2,1)S(1)}, u32[]{:S(2)}, u32[]{:S(2)}) async-start(bf16[32,64,256]{2,1,0:T(8,128)(2,1)} %bitcast.11), calls=%async_computation | async-start | bytes 2097152 | tf_op jit(solution)/shard_map/all_to_all | solution.py:524
  34.7 3.3 %collective-permute-done.5.refs_2_ = f32[1,1,4096]{2,1,0:T(1,128)S(1)} collective-permute-done((f32[1,1,4096]{2,1,0:T(1,128)S(1)}, f32[1,1,4096]{2,1,0:T(1,128)S(1)}, u32[]{:S(2)}, u32[]{:S(2)}) %collective-permute-start.5) | collective-permute-done | bytes 16416 | tf_op jit(solution)/shard_map/ppermute | solution.py:496
  46.1 3.5 %collective-permute-start.10 = (f32[1,1,4096]{2,1,0:T(1,128)S(1)}, f32[1,1,4096]{2,1,0:T(1,128)S(1)}, u32[]{:S(2)}, u32[]{:S(2)}) collective-permute-start(f32[1,1,4096]{2,1,0:T(1,128)S(1)} %add.8.refs_0_), channel_id=1, source_target_pairs={{0,4},{1,5},{2,6},{3,7},{4,0},{5,1},{6,2},{7,3},{8,12},{9,13},{10,... | collective-permute-start | bytes 49160 | tf_op jit(solution)/shard_map/ppermute | solution.py:496
  52.7 6.0 %cg_load.1 = (bf16[1024,4096]{1,0:T(8,128)(2,1)S(1)}, f32[16,1,4096]{2,1,0:T(1,128)S(1)}, f32[1,4096]{1,0:T(1,128)S(1)}, f32[1,128]{1,0:T(1,128)S(1)}, f32[1,1024]{1,0:T(1,128)S(1)}) custom-call(bf16[1024,4096]{1,0:T(8,128)(2,1)} %x_hbm.3, f32[1,1,4096]{2,1,0:T(1,128)S(1)} %add.9.sum_ref, f32[1,4096]{1,0:T(1,128)S(1)} %get-tuple-element.59.scale_ref, ...), custom_call_target="tpu_custom_call" | custom-call | tf_op jit(solution)/shard_map/cg_load/pallas_call | solution.py:532
  58.8 17.1 %all_to_all.75.sum_ref = f32[16,1,4096]{2,1,0:T(1,128)S(1)} all-to-all(f32[16,1,4096]{2,1,0:T(1,128)S(1)} %get-tuple-element.63), channel_id=1, replica_groups=mesh['x'=4,'core'=2,'y'=4,'z'=8] {'core','z'}, dimensions={0} | all-to-all | bytes 524288 | tf_op jit(solution)/shard_map/all_to_all | solution.py:484
  75.9 13.9 %all_to_all.76.sum_ref = f32[16,1,4096]{2,1,0:T(1,128)S(1)} all-to-all(f32[16,1,4096]{2,1,0:T(1,128)S(1)} %again.5), channel_id=1, replica_groups=mesh['x'=4,'core'=2,'y'=4,'z'=8] {'x','y'}, dimensions={0} | all-to-all | bytes 524288 | tf_op jit(solution)/shard_map/all_to_all | solution.py:484
  89.8 4.2 %cg_next.2 = (f32[16,1,4096]{2,1,0:T(1,128)S(1)}, f32[1,4096]{1,0:T(1,128)S(1)}, f32[1,4096]{1,0:T(1,128)S(1)}, f32[1,4096]{1,0:T(1,128)S(1)}, f32[1,128]{1,0:T(...) custom-call(bf16[1024,4096]{1,0:T(8,128)(2,1)S(1)} %get-tuple-element.62.x_ref, ...), custom_call_target="tpu_custom_call" | custom-call | tf_op jit(solution)/shard_map/cg_next/pallas_call | solution.py:458
  94.1 16.0 %all_to_all.77.sum_ref = f32[16,1,4096]{2,1,0:T(1,128)S(1)} all-to-all(f32[16,1,4096]{2,1,0:T(1,128)S(1)} %get-tuple-element.67), channel_id=1, replica_groups=mesh['x'=4,'core'=2,'y'=4,'z'=8] {'core','z'}, dimensions={0} | all-to-all | bytes 524288 | tf_op jit(solution)/shard_map/all_to_all | solution.py:484
  110.1 10.5 %all_to_all.78.sum_ref = f32[16,1,4096]{2,1,0:T(1,128)S(1)} all-to-all(f32[16,1,4096]{2,1,0:T(1,128)S(1)} %again.6), channel_id=1, replica_groups=mesh['x'=4,'core'=2,'y'=4,'z'=8] {'x','y'}, dimensions={0} | all-to-all | bytes 524288 | tf_op jit(solution)/shard_map/all_to_all | solution.py:484
  123.9 22.0 %all_to_all.79.part_ref = f32[256,1,128]{2,1,0:T(1,128)S(1)} all-to-all(f32[256,1,128]{2,1,0:T(1,128)S(1)} %get-tuple-element.74), channel_id=1, replica_groups=mesh['x'=4,'core'=2,'y'=4,'z'=8] {'x','core','y','z'}, dimensions={0} | all-to-all | bytes 262144 | tf_op jit(solution)/shard_map/all_to_all | solution.py:484
  147.5 12.4 %all_to_all.80.sum_ref = f32[16,1,4096]{2,1,0:T(1,128)S(1)} all-to-all(f32[16,1,4096]{2,1,0:T(1,128)S(1)} %get-tuple-element.83), channel_id=1, replica_groups=mesh['x'=4,'core'=2,'y'=4,'z'=8] {'core','z'}, dimensions={0} | all-to-all | bytes 524288 | tf_op jit(solution)/shard_map/all_to_all | solution.py:484
  159.9 10.3 %all_to_all.81.sum_ref = f32[16,1,4096]{2,1,0:T(1,128)S(1)} all-to-all(f32[16,1,4096]{2,1,0:T(1,128)S(1)} %again.7), channel_id=1, replica_groups=mesh['x'=4,'core'=2,'y'=4,'z'=8] {'x','y'}, dimensions={0} | all-to-all | bytes 524288 | tf_op jit(solution)/shard_map/all_to_all | solution.py:484
  170.2 3.9 %cg_first.1 = (f32[16,1,4096]{2,1,0:T(1,128)S(1)}, f32[1,4096]{1,0:T(1,128)S(1)}, f32[1,128]{1,0:T(1,128)S(1)}, f32[1,1024]{1,0:T(1,128)S(1)}) custom-call(bf16[1024,4096]{1,0:T(8,128)(2,1)S(1)} %get-tuple-element.62.x_ref, f32[16,1,4096]{2,1,0:T(1,128)S(1)} %all_to_all.81.sum_ref, f32[1,4096]{1,0:T(1,128)S(1)} %get-tuple-element.59.scale_ref, ...), custom_call_target="tpu_custom_call" | custom-call | tf_op jit(solution)/shard_map/cg_first/pallas_call | solution.py:458
  174.1 16.0 %all_to_all.82.sum_ref = f32[16,1,4096]{2,1,0:T(1,128)S(1)} all-to-all(f32[16,1,4096]{2,1,0:T(1,128)S(1)} %get-tuple-element.86), channel_id=1, replica_groups=mesh['x'=4,'core'=2,'y'=4,'z'=8] {'core','z'}, dimensions={0} | all-to-all | bytes 524288 | tf_op jit(solution)/shard_map/all_to_all | solution.py:484
  190.2 10.5 %all_to_all.83.sum_ref = f32[16,1,4096]{2,1,0:T(1,128)S(1)} all-to-all(f32[16,1,4096]{2,1,0:T(1,128)S(1)} %again.8), channel_id=1, replica_groups=mesh['x'=4,'core'=2,'y'=4,'z'=8] {'x','y'}, dimensions={0} | all-to-all | bytes 524288 | tf_op jit(solution)/shard_map/all_to_all | solution.py:484
  200.7 4.2 %cg_next.3 = (f32[16,1,4096]{2,1,0:T(1,128)S(1)}, f32[1,4096]{1,0:T(1,128)S(1)}, f32[1,4096]{1,0:T(1,128)S(1)}, f32[1,4096]{1,0:T(1,128)S(1)}, f32[1,128]{1,0:T(...) custom-call(bf16[1024,4096]{1,0:T(8,128)(2,1)S(1)} %get-tuple-element.62.x_ref, ...), custom_call_target="tpu_custom_call" | custom-call | tf_op jit(solution)/shard_map/cg_next/pallas_call | solution.py:458
  204.9 16.0 %all_to_all.84.sum_ref = f32[16,1,4096]{2,1,0:T(1,128)S(1)} all-to-all(f32[16,1,4096]{2,1,0:T(1,128)S(1)} %get-tuple-element.90), channel_id=1, replica_groups=mesh['x'=4,'core'=2,'y'=4,'z'=8] {'core','z'}, dimensions={0} | all-to-all | bytes 524288 | tf_op jit(solution)/shard_map/all_to_all | solution.py:484
  221.0 10.5 %all_to_all.85.sum_ref = f32[16,1,4096]{2,1,0:T(1,128)S(1)} all-to-all(f32[16,1,4096]{2,1,0:T(1,128)S(1)} %again.9), channel_id=1, replica_groups=mesh['x'=4,'core'=2,'y'=4,'z'=8] {'x','y'}, dimensions={0} | all-to-all | bytes 524288 | tf_op jit(solution)/shard_map/all_to_all | solution.py:484
  231.5 3.7 %cg_last_pack.1 = (f32[32,1,256]{2,1,0:T(1,128)S(1)}, f32[1,4096]{1,0:T(1,128)S(1)}, f32[1,4096]{1,0:T(1,128)S(1)}, f32[1,128]{1,0:T(1,128)S(1)}) custom-call(bf16[1024,4096]{1,0:T(8,128)(2,1)S(1)} %get-tuple-element.62.x_ref, f32[16,1,4096]{2,1,0:T(1,128)S(1)} %all_to_all.85.sum_ref, f32[1,4096]{1,0:T(1,128)S(1)} %get-tuple-element.59.scale_ref, ...), custom_call_target="tpu_custom_call" | custom-call | tf_op jit(solution)/shard_map/cg_last_pack/pallas_call | solution.py:458
  235.2 15.1 %all_to_all.86.arr_ref = f32[32,1,256]{2,1,0:T(1,128)S(1)} all-to-all(f32[32,1,256]{2,1,0:T(1,128)S(1)} %get-tuple-element.100), channel_id=1, replica_groups=mesh['x'=4,'core'=2,'y'=4,'z'=8] {'y','z'}, dimensions={0} | all-to-all | bytes 65536 | tf_op jit(solution)/shard_map/all_to_all | solution.py:484
  250.4 9.7 %all_to_all.87.part_ref = f32[8,1,128]{2,1,0:T(1,128)S(1)} all-to-all(f32[8,1,128]{2,1,0:T(1,128)S(1)} %part.1), channel_id=1, replica_groups=mesh['x'=4,'core'=2,'y'=4,'z'=8] {'x','core'}, dimensions={0} | all-to-all | bytes 8192 | tf_op jit(solution)/shard_map/all_to_all | solution.py:484
  260.1 20.4 %members.1 = (f32[1,4096]{1,0:T(1,128)}, f32[8,256]{1,0:T(8,128)}, f32[32,1,64]{2,1,0:T(1,128)S(1)}) custom-call(bf16[2048,256]{1,0:T(8,128)(2,1)} %bitcast.10, f32[32,1,256]{2,1,0:T(1,128)S(1)} %all_to_all.86.arr_ref, f32[8,1,128]{2,1,0:T(1,128)S(1)} %all_to_all.87.part_ref, f32[1,128]{1,0:T(1,128)S(1)} %get-tuple-element.101.rr_ref, ...), custom_call_target="tpu_custom_call" | custom-call | tf_op jit(solution)/shard_map/members/pallas_call | solution.py:568
  280.5 11.6 %all_to_all.88.back_ref = f32[32,1,64]{2,1,0:T(1,128)S(1)} all-to-all(f32[32,1,64]{2,1,0:T(1,128)S(1)} %get-tuple-element.106), channel_id=1, replica_groups=mesh['x'=4,'core'=2,'y'=4,'z'=8] {'y','z'}, dimensions={0} | all-to-all | bytes 16384 | tf_op jit(solution)/shard_map/all_to_all | solution.py:484
  (37 shorter events, 31.6 us)
Async XLA Ops:
  8.4 44.3 %all-to-all-start = ((bf16[32,64,256]{2,1,0:T(8,128)(2,1)}), bf16[32,64,256]{2,1,0:T(8,128)(2,1)S(1)}, u32[]{:S(2)}, u32[]{:S(2)}) async-start(bf16[32,64,256]{2,1,0:T(8,128)(2,1)} %bitcast.11), calls=%async_computation | async-start | bytes 2097152 | tf_op jit(solution)/shard_map/all_to_all | solution.py:524
  20.5 3.9 %collective-permute-start.2 = (f32[1,1,4096]{2,1,0:T(1,128)S(1)}, f32[1,1,4096]{2,1,0:T(1,128)S(1)}, u32[]{:S(2)}, u32[]{:S(2)}) collective-permute-start(f32[1,1,4096]{2,1,0:T(1,128)S(1)} %get-tuple-element.55.refs_0_), channel_id=1, source_target_pairs={{0,192},{64,128},{128,64},{192,0},{1,193},{65,129},{129,65},{193,1... | collective-permute-start | bytes 49160 | tf_op jit(solution)/shard_map/ppermute | solution.py:496
  23.0 4.1 %collective-permute-start.1 = (f32[1,1,4096]{2,1,0:T(1,128)S(1)}, f32[1,1,4096]{2,1,0:T(1,128)S(1)}, u32[]{:S(2)}, u32[]{:S(2)}) collective-permute-start(f32[1,1,4096]{2,1,0:T(1,128)S(1)} %get-tuple-element.55.refs_0_), channel_id=1, source_target_pairs={{0,128},{64,192},{128,0},{192,64},{1,129},{65,193},{129,1},{193,65... | collective-permute-start | bytes 49160 | tf_op jit(solution)/shard_map/ppermute | solution.py:496
  23.6 3.6 %collective-permute-start = (f32[1,1,4096]{2,1,0:T(1,128)S(1)}, f32[1,1,4096]{2,1,0:T(1,128)S(1)}, u32[]{:S(2)}, u32[]{:S(2)}) collective-permute-start(f32[1,1,4096]{2,1,0:T(1,128)S(1)} %get-tuple-element.55.refs_0_), channel_id=1, source_target_pairs={{0,64},{64,0},{128,192},{192,128},{1,65},{65,1},{129,193},{193,129... | collective-permute-start | bytes 49160 | tf_op jit(solution)/shard_map/ppermute | solution.py:496
  27.2 3.3 %collective-permute-start.3 = (f32[1,1,4096]{2,1,0:T(1,128)S(1)}, f32[1,1,4096]{2,1,0:T(1,128)S(1)}, u32[]{:S(2)}, u32[]{:S(2)}) collective-permute-start(f32[1,1,4096]{2,1,0:T(1,128)S(1)} %add.5.refs_0_), channel_id=1, source_target_pairs={{0,32},{32,0},{1,33},{33,1},{2,34},{34,2},{3,35},{35,3},{4,36},{36... | collective-permute-start | bytes 49160 | tf_op jit(solution)/shard_map/ppermute | solution.py:496
  30.5 4.2 %collective-permute-start.6 = (f32[1,1,4096]{2,1,0:T(1,128)S(1)}, f32[1,1,4096]{2,1,0:T(1,128)S(1)}, u32[]{:S(2)}, u32[]{:S(2)}) collective-permute-start(f32[1,1,4096]{2,1,0:T(1,128)S(1)} %add.6.refs_0_), channel_id=1, source_target_pairs={{0,24},{8,16},{16,8},{24,0},{1,25},{9,17},{17,9},{25,1},{2,26},{10... | collective-permute-start | bytes 49160 | tf_op jit(solution)/shard_map/ppermute | solution.py:496
  33.2 4.7 %collective-permute-start.5 = (f32[1,1,4096]{2,1,0:T(1,128)S(1)}, f32[1,1,4096]{2,1,0:T(1,128)S(1)}, u32[]{:S(2)}, u32[]{:S(2)}) collective-permute-start(f32[1,1,4096]{2,1,0:T(1,128)S(1)} %add.6.refs_0_), channel_id=1, source_target_pairs={{0,16},{8,24},{16,0},{24,8},{1,17},{9,25},{17,1},{25,9},{2,18},{10... | collective-permute-start | bytes 49160 | tf_op jit(solution)/shard_map/ppermute | solution.py:496
  33.8 4.2 %collective-permute-start.4 = (f32[1,1,4096]{2,1,0:T(1,128)S(1)}, f32[1,1,4096]{2,1,0:T(1,128)S(1)}, u32[]{:S(2)}, u32[]{:S(2)}) collective-permute-start(f32[1,1,4096]{2,1,0:T(1,128)S(1)} %add.6.refs_0_), channel_id=1, source_target_pairs={{0,8},{8,0},{16,24},{24,16},{1,9},{9,1},{17,25},{25,17},{2,10},{10... | collective-permute-start | bytes 49160 | tf_op jit(solution)/shard_map/ppermute | solution.py:496
  38.0 5.1 %collective-permute-start.9 = (f32[1,1,4096]{2,1,0:T(1,128)S(1)}, f32[1,1,4096]{2,1,0:T(1,128)S(1)}, u32[]{:S(2)}, u32[]{:S(2)}) collective-permute-start(f32[1,1,4096]{2,1,0:T(1,128)S(1)} %add.7.refs_0_), channel_id=1, source_target_pairs={{0,3},{1,2},{2,1},{3,0},{4,7},{5,6},{6,5},{7,4},{8,11},{9,10},{10,... | collective-permute-start | bytes 49160 | tf_op jit(solution)/shard_map/ppermute | solution.py:496
  40.9 5.2 %collective-permute-start.8 = (f32[1,1,4096]{2,1,0:T(1,128)S(1)}, f32[1,1,4096]{2,1,0:T(1,128)S(1)}, u32[]{:S(2)}, u32[]{:S(2)}) collective-permute-start(f32[1,1,4096]{2,1,0:T(1,128)S(1)} %add.7.refs_0_), channel_id=1, source_target_pairs={{0,2},{1,3},{2,0},{3,1},{4,6},{5,7},{6,4},{7,5},{8,10},{9,11},{10,... | collective-permute-start | bytes 49160 | tf_op jit(solution)/shard_map/ppermute | solution.py:496
  40.9 5.2 %collective-permute-start.7 = (f32[1,1,4096]{2,1,0:T(1,128)S(1)}, f32[1,1,4096]{2,1,0:T(1,128)S(1)}, u32[]{:S(2)}, u32[]{:S(2)}) collective-permute-start(f32[1,1,4096]{2,1,0:T(1,128)S(1)} %add.7.refs_0_), channel_id=1, source_target_pairs={{0,1},{1,0},{2,3},{3,2},{4,5},{5,4},{6,7},{7,6},{8,9},{9,8},{10,11... | collective-permute-start | bytes 49160 | tf_op jit(solution)/shard_map/ppermute | solution.py:496
  46.1 6.6 %collective-permute-start.10 = (f32[1,1,4096]{2,1,0:T(1,128)S(1)}, f32[1,1,4096]{2,1,0:T(1,128)S(1)}, u32[]{:S(2)}, u32[]{:S(2)}) collective-permute-start(f32[1,1,4096]{2,1,0:T(1,128)S(1)} %add.8.refs_0_), channel_id=1, source_target_pairs={{0,4},{1,5},{2,6},{3,7},{4,0},{5,1},{6,2},{7,3},{8,12},{9,13},{10,... | collective-permute-start | bytes 49160 | tf_op jit(solution)/shard_map/ppermute | solution.py:496
  52.7 41.3 %copy-start = (bf16[32,64,256]{2,1,0:T(8,128)(2,1)}, bf16[32,64,256]{2,1,0:T(8,128)(2,1)S(1)}, u32[]{:S(2)}) copy-start(bf16[32,64,256]{2,1,0:T(8,128)(2,1)S(1)} %all-to-all-done) | copy-start | bytes 3145732

commit v4 on v3

--- a/solution.py
+++ b/solution.py
@@ -466,14 +466,14 @@
     )(*ins)
 
 
-PH1 = ("core", "z")
-PH2 = ("x", "y")
+PH1 = ("x", "y")
+PH2 = ("core", "z")
 
 
 def on_device(features, re_features, member_id, slot, labels, offsets, feature_scale, w_start,
               *, sizes):
-    n1 = sizes["core"] * sizes["z"]
-    n2 = sizes["x"] * sizes["y"]
+    n1 = sizes["x"] * sizes["y"]
+    n2 = sizes["core"] * sizes["z"]
     n_mem = sizes["y"] * sizes["z"]
     n_grp = sizes["x"] * sizes["core"]
     rows, f = features.shape

time: 294 us -> 293 us (level)
  no operation moved by 1% of the time
where the time goes in v4:
time: 293 us
  blocking collectives  191 us (65%)
  Pallas kernels  56.4 us (19%)
  starting transfers between devices  28.4 us (10%)
  waiting for transfers between devices  15.9 us (5%)
    all_to_all x14, blocking collectives, exchange(): return lax.all_to_all(v, axes, 0, 0, tiled=True)  191 us
    pallas_call x17, Pallas kernels, on_chip(): pl.pallas_call(kernel, in_specs=[vmem] * len(ins), out_specs=[vmem] * len...  21.2 us
    pallas_call x1, Pallas kernels, on_device(): pl.pallas_call(member_kernel, in_specs=[pl.BlockSpec(memory_space=pltpu.H...  20.4 us
    ppermute x11, starting transfers between devices, reduce_permutes(): lax.ppermute(v, axis, [(i, i ^ b) for i in range(size)])  16.3 us
    ppermute x11, waiting for transfers between devices, reduce_permutes(): lax.ppermute(v, axis, [(i, i ^ b) for i in range(size)])  15.9 us
    all_to_all x1, starting transfers between devices, on_device(): lax.all_to_all(packed.reshape(n_mem, cap, fr), ('y', 'z'), 0, 0, tiled=True)  12 us
    pallas_call x1, Pallas kernels, on_device(): pl.pallas_call(start_kernel, in_specs=[hbm] * 8, out_specs=[hbm] + [vmem]...  7.79 us
    pallas_call x1, Pallas kernels, on_device(): pl.pallas_call(cg_load_kernel, in_specs=[hbm] + [vmem] * 4, out_specs=[vm...  6.04 us
  transfers between devices with their start and end apart: 12, of which 8 were waited for; matrix products, arithmetic and copies ran while one was open for 0% of the time, Pallas kernels for 0%

profile of v4, /device:TPU:1, one launch (start us, length us, event | category | flops | bytes accessed | tf_op | source)
XLA Modules:
  0.0 292.7 jit_solution(16221569706770897157)
XLA Ops:
  0.6 7.8 %start.1 = (bf16[2048,256]{1,0:T(8,128)(2,1)}, s32[1,1024]{1,0:T(1,128)S(1)}, f32[1,1024]{1,0:T(1,128)S(1)}, f32[1,1024]{1,0:T(1,128)S(1)}, f32[1,1024]{1,0:T(1,...) custom-call(bf16[1024,4096]{1,0:T(8,128)(2,1)} %x_hbm.3, ...), custom_call_target="tpu_custom_call" | custom-call | tf_op jit(solution)/shard_map/start/pallas_call | solution.py:509
  8.4 12.0 %all-to-all-start = ((bf16[32,64,256]{2,1,0:T(8,128)(2,1)}), bf16[32,64,256]{2,1,0:T(8,128)(2,1)S(1)}, u32[]{:S(2)}, u32[]{:S(2)}) async-start(bf16[32,64,256]{2,1,0:T(8,128)(2,1)} %bitcast.11), calls=%async_computation | async-start | bytes 2097152 | tf_op jit(solution)/shard_map/all_to_all | solution.py:524
  34.7 3.3 %collective-permute-done.5.refs_2_ = f32[1,1,4096]{2,1,0:T(1,128)S(1)} collective-permute-done((f32[1,1,4096]{2,1,0:T(1,128)S(1)}, f32[1,1,4096]{2,1,0:T(1,128)S(1)}, u32[]{:S(2)}, u32[]{:S(2)}) %collective-permute-start.5) | collective-permute-done | bytes 16416 | tf_op jit(solution)/shard_map/ppermute | solution.py:496
  46.1 3.5 %collective-permute-start.10 = (f32[1,1,4096]{2,1,0:T(1,128)S(1)}, f32[1,1,4096]{2,1,0:T(1,128)S(1)}, u32[]{:S(2)}, u32[]{:S(2)}) collective-permute-start(f32[1,1,4096]{2,1,0:T(1,128)S(1)} %add.8.refs_0_), channel_id=1, source_target_pairs={{0,4},{1,5},{2,6},{3,7},{4,0},{5,1},{6,2},{7,3},{8,12},{9,13},{10,... | collective-permute-start | bytes 49160 | tf_op jit(solution)/shard_map/ppermute | solution.py:496
  52.7 6.0 %cg_load.1 = (bf16[1024,4096]{1,0:T(8,128)(2,1)S(1)}, f32[16,1,4096]{2,1,0:T(1,128)S(1)}, f32[1,4096]{1,0:T(1,128)S(1)}, f32[1,128]{1,0:T(1,128)S(1)}, f32[1,1024]{1,0:T(1,128)S(1)}) custom-call(bf16[1024,4096]{1,0:T(8,128)(2,1)} %x_hbm.3, f32[1,1,4096]{2,1,0:T(1,128)S(1)} %add.9.sum_ref, f32[1,4096]{1,0:T(1,128)S(1)} %get-tuple-element.59.scale_ref, ...), custom_call_target="tpu_custom_call" | custom-call | tf_op jit(solution)/shard_map/cg_load/pallas_call | solution.py:532
  58.8 12.2 %all_to_all.75.sum_ref = f32[16,1,4096]{2,1,0:T(1,128)S(1)} all-to-all(f32[16,1,4096]{2,1,0:T(1,128)S(1)} %get-tuple-element.63), channel_id=1, replica_groups=mesh['x'=4,'core'=2,'y'=4,'z'=8] {'x','y'}, dimensions={0} | all-to-all | bytes 524288 | tf_op jit(solution)/shard_map/all_to_all | solution.py:484
  71.0 20.2 %all_to_all.76.sum_ref = f32[16,1,4096]{2,1,0:T(1,128)S(1)} all-to-all(f32[16,1,4096]{2,1,0:T(1,128)S(1)} %again.5), channel_id=1, replica_groups=mesh['x'=4,'core'=2,'y'=4,'z'=8] {'core','z'}, dimensions={0} | all-to-all | bytes 524288 | tf_op jit(solution)/shard_map/all_to_all | solution.py:484
  91.3 4.2 %cg_next.2 = (f32[16,1,4096]{2,1,0:T(1,128)S(1)}, f32[1,4096]{1,0:T(1,128)S(1)}, f32[1,4096]{1,0:T(1,128)S(1)}, f32[1,4096]{1,0:T(1,128)S(1)}, f32[1,128]{1,0:T(...) custom-call(bf16[1024,4096]{1,0:T(8,128)(2,1)S(1)} %get-tuple-element.62.x_ref, ...), custom_call_target="tpu_custom_call" | custom-call | tf_op jit(solution)/shard_map/cg_next/pallas_call | solution.py:458
  95.5 10.5 %all_to_all.77.sum_ref = f32[16,1,4096]{2,1,0:T(1,128)S(1)} all-to-all(f32[16,1,4096]{2,1,0:T(1,128)S(1)} %get-tuple-element.67), channel_id=1, replica_groups=mesh['x'=4,'core'=2,'y'=4,'z'=8] {'x','y'}, dimensions={0} | all-to-all | bytes 524288 | tf_op jit(solution)/shard_map/all_to_all | solution.py:484
  106.1 16.0 %all_to_all.78.sum_ref = f32[16,1,4096]{2,1,0:T(1,128)S(1)} all-to-all(f32[16,1,4096]{2,1,0:T(1,128)S(1)} %again.6), channel_id=1, replica_groups=mesh['x'=4,'core'=2,'y'=4,'z'=8] {'core','z'}, dimensions={0} | all-to-all | bytes 524288 | tf_op jit(solution)/shard_map/all_to_all | solution.py:484
  125.4 20.3 %all_to_all.79.part_ref = f32[256,1,128]{2,1,0:T(1,128)S(1)} all-to-all(f32[256,1,128]{2,1,0:T(1,128)S(1)} %get-tuple-element.74), channel_id=1, replica_groups=mesh['x'=4,'core'=2,'y'=4,'z'=8] {'x','core','y','z'}, dimensions={0} | all-to-all | bytes 262144 | tf_op jit(solution)/shard_map/all_to_all | solution.py:484
  147.3 10.0 %all_to_all.80.sum_ref = f32[16,1,4096]{2,1,0:T(1,128)S(1)} all-to-all(f32[16,1,4096]{2,1,0:T(1,128)S(1)} %get-tuple-element.83), channel_id=1, replica_groups=mesh['x'=4,'core'=2,'y'=4,'z'=8] {'x','y'}, dimensions={0} | all-to-all | bytes 524288 | tf_op jit(solution)/shard_map/all_to_all | solution.py:484
  157.4 14.1 %all_to_all.81.sum_ref = f32[16,1,4096]{2,1,0:T(1,128)S(1)} all-to-all(f32[16,1,4096]{2,1,0:T(1,128)S(1)} %again.7), channel_id=1, replica_groups=mesh['x'=4,'core'=2,'y'=4,'z'=8] {'core','z'}, dimensions={0} | all-to-all | bytes 524288 | tf_op jit(solution)/shard_map/all_to_all | solution.py:484
  171.5 3.9 %cg_first.1 = (f32[16,1,4096]{2,1,0:T(1,128)S(1)}, f32[1,4096]{1,0:T(1,128)S(1)}, f32[1,128]{1,0:T(1,128)S(1)}, f32[1,1024]{1,0:T(1,128)S(1)}) custom-call(bf16[1024,4096]{1,0:T(8,128)(2,1)S(1)} %get-tuple-element.62.x_ref, f32[16,1,4096]{2,1,0:T(1,128)S(1)} %all_to_all.81.sum_ref, f32[1,4096]{1,0:T(1,128)S(1)} %get-tuple-element.59.scale_ref, ...), custom_call_target="tpu_custom_call" | custom-call | tf_op jit(solution)/shard_map/cg_first/pallas_call | solution.py:458
  175.4 10.5 %all_to_all.82.sum_ref = f32[16,1,4096]{2,1,0:T(1,128)S(1)} all-to-all(f32[16,1,4096]{2,1,0:T(1,128)S(1)} %get-tuple-element.86), channel_id=1, replica_groups=mesh['x'=4,'core'=2,'y'=4,'z'=8] {'x','y'}, dimensions={0} | all-to-all | bytes 524288 | tf_op jit(solution)/shard_map/all_to_all | solution.py:484
  185.9 16.0 %all_to_all.83.sum_ref = f32[16,1,4096]{2,1,0:T(1,128)S(1)} all-to-all(f32[16,1,4096]{2,1,0:T(1,128)S(1)} %again.8), channel_id=1, replica_groups=mesh['x'=4,'core'=2,'y'=4,'z'=8] {'core','z'}, dimensions={0} | all-to-all | bytes 524288 | tf_op jit(solution)/shard_map/all_to_all | solution.py:484
  202.0 4.2 %cg_next.3 = (f32[16,1,4096]{2,1,0:T(1,128)S(1)}, f32[1,4096]{1,0:T(1,128)S(1)}, f32[1,4096]{1,0:T(1,128)S(1)}, f32[1,4096]{1,0:T(1,128)S(1)}, f32[1,128]{1,0:T(...) custom-call(bf16[1024,4096]{1,0:T(8,128)(2,1)S(1)} %get-tuple-element.62.x_ref, ...), custom_call_target="tpu_custom_call" | custom-call | tf_op jit(solution)/shard_map/cg_next/pallas_call | solution.py:458
  206.2 10.5 %all_to_all.84.sum_ref = f32[16,1,4096]{2,1,0:T(1,128)S(1)} all-to-all(f32[16,1,4096]{2,1,0:T(1,128)S(1)} %get-tuple-element.90), channel_id=1, replica_groups=mesh['x'=4,'core'=2,'y'=4,'z'=8] {'x','y'}, dimensions={0} | all-to-all | bytes 524288 | tf_op jit(solution)/shard_map/all_to_all | solution.py:484
  216.7 16.0 %all_to_all.85.sum_ref = f32[16,1,4096]{2,1,0:T(1,128)S(1)} all-to-all(f32[16,1,4096]{2,1,0:T(1,128)S(1)} %again.9), channel_id=1, replica_groups=mesh['x'=4,'core'=2,'y'=4,'z'=8] {'core','z'}, dimensions={0} | all-to-all | bytes 524288 | tf_op jit(solution)/shard_map/all_to_all | solution.py:484
  232.7 3.7 %cg_last_pack.1 = (f32[32,1,256]{2,1,0:T(1,128)S(1)}, f32[1,4096]{1,0:T(1,128)S(1)}, f32[1,4096]{1,0:T(1,128)S(1)}, f32[1,128]{1,0:T(1,128)S(1)}) custom-call(bf16[1024,4096]{1,0:T(8,128)(2,1)S(1)} %get-tuple-element.62.x_ref, f32[16,1,4096]{2,1,0:T(1,128)S(1)} %all_to_all.85.sum_ref, f32[1,4096]{1,0:T(1,128)S(1)} %get-tuple-element.59.scale_ref, ...), custom_call_target="tpu_custom_call" | custom-call | tf_op jit(solution)/shard_map/cg_last_pack/pallas_call | solution.py:458
  236.5 14.3 %all_to_all.86.arr_ref = f32[32,1,256]{2,1,0:T(1,128)S(1)} all-to-all(f32[32,1,256]{2,1,0:T(1,128)S(1)} %get-tuple-element.100), channel_id=1, replica_groups=mesh['x'=4,'core'=2,'y'=4,'z'=8] {'y','z'}, dimensions={0} | all-to-all | bytes 65536 | tf_op jit(solution)/shard_map/all_to_all | solution.py:484
  250.8 8.9 %all_to_all.87.part_ref = f32[8,1,128]{2,1,0:T(1,128)S(1)} all-to-all(f32[8,1,128]{2,1,0:T(1,128)S(1)} %part.1), channel_id=1, replica_groups=mesh['x'=4,'core'=2,'y'=4,'z'=8] {'x','core'}, dimensions={0} | all-to-all | bytes 8192 | tf_op jit(solution)/shard_map/all_to_all | solution.py:484
  259.7 20.4 %members.1 = (f32[1,4096]{1,0:T(1,128)}, f32[8,256]{1,0:T(8,128)}, f32[32,1,64]{2,1,0:T(1,128)S(1)}) custom-call(bf16[2048,256]{1,0:T(8,128)(2,1)} %bitcast.10, f32[32,1,256]{2,1,0:T(1,128)S(1)} %all_to_all.86.arr_ref, f32[8,1,128]{2,1,0:T(1,128)S(1)} %all_to_all.87.part_ref, f32[1,128]{1,0:T(1,128)S(1)} %get-tuple-element.101.rr_ref, ...), custom_call_target="tpu_custom_call" | custom-call | tf_op jit(solution)/shard_map/members/pallas_call | solution.py:568
  280.1 11.6 %all_to_all.88.back_ref = f32[32,1,64]{2,1,0:T(1,128)S(1)} all-to-all(f32[32,1,64]{2,1,0:T(1,128)S(1)} %get-tuple-element.106), channel_id=1, replica_groups=mesh['x'=4,'core'=2,'y'=4,'z'=8] {'y','z'}, dimensions={0} | all-to-all | bytes 16384 | tf_op jit(solution)/shard_map/all_to_all | solution.py:484
  (37 shorter events, 31.6 us)
Async XLA Ops:
  8.4 44.3 %all-to-all-start = ((bf16[32,64,256]{2,1,0:T(8,128)(2,1)}), bf16[32,64,256]{2,1,0:T(8,128)(2,1)S(1)}, u32[]{:S(2)}, u32[]{:S(2)}) async-start(bf16[32,64,256]{2,1,0:T(8,128)(2,1)} %bitcast.11), calls=%async_computation | async-start | bytes 2097152 | tf_op jit(solution)/shard_map/all_to_all | solution.py:524
  20.5 3.9 %collective-permute-start.2 = (f32[1,1,4096]{2,1,0:T(1,128)S(1)}, f32[1,1,4096]{2,1,0:T(1,128)S(1)}, u32[]{:S(2)}, u32[]{:S(2)}) collective-permute-start(f32[1,1,4096]{2,1,0:T(1,128)S(1)} %get-tuple-element.55.refs_0_), channel_id=1, source_target_pairs={{0,192},{64,128},{128,64},{192,0},{1,193},{65,129},{129,65},{193,1... | collective-permute-start | bytes 49160 | tf_op jit(solution)/shard_map/ppermute | solution.py:496
  23.0 4.1 %collective-permute-start.1 = (f32[1,1,4096]{2,1,0:T(1,128)S(1)}, f32[1,1,4096]{2,1,0:T(1,128)S(1)}, u32[]{:S(2)}, u32[]{:S(2)}) collective-permute-start(f32[1,1,4096]{2,1,0:T(1,128)S(1)} %get-tuple-element.55.refs_0_), channel_id=1, source_target_pairs={{0,128},{64,192},{128,0},{192,64},{1,129},{65,193},{129,1},{193,65... | collective-permute-start | bytes 49160 | tf_op jit(solution)/shard_map/ppermute | solution.py:496
  23.6 3.6 %collective-permute-start = (f32[1,1,4096]{2,1,0:T(1,128)S(1)}, f32[1,1,4096]{2,1,0:T(1,128)S(1)}, u32[]{:S(2)}, u32[]{:S(2)}) collective-permute-start(f32[1,1,4096]{2,1,0:T(1,128)S(1)} %get-tuple-element.55.refs_0_), channel_id=1, source_target_pairs={{0,64},{64,0},{128,192},{192,128},{1,65},{65,1},{129,193},{193,129... | collective-permute-start | bytes 49160 | tf_op jit(solution)/shard_map/ppermute | solution.py:496
  27.2 3.3 %collective-permute-start.3 = (f32[1,1,4096]{2,1,0:T(1,128)S(1)}, f32[1,1,4096]{2,1,0:T(1,128)S(1)}, u32[]{:S(2)}, u32[]{:S(2)}) collective-permute-start(f32[1,1,4096]{2,1,0:T(1,128)S(1)} %add.5.refs_0_), channel_id=1, source_target_pairs={{0,32},{32,0},{1,33},{33,1},{2,34},{34,2},{3,35},{35,3},{4,36},{36... | collective-permute-start | bytes 49160 | tf_op jit(solution)/shard_map/ppermute | solution.py:496
  30.5 4.2 %collective-permute-start.6 = (f32[1,1,4096]{2,1,0:T(1,128)S(1)}, f32[1,1,4096]{2,1,0:T(1,128)S(1)}, u32[]{:S(2)}, u32[]{:S(2)}) collective-permute-start(f32[1,1,4096]{2,1,0:T(1,128)S(1)} %add.6.refs_0_), channel_id=1, source_target_pairs={{0,24},{8,16},{16,8},{24,0},{1,25},{9,17},{17,9},{25,1},{2,26},{10... | collective-permute-start | bytes 49160 | tf_op jit(solution)/shard_map/ppermute | solution.py:496
  33.2 4.7 %collective-permute-start.5 = (f32[1,1,4096]{2,1,0:T(1,128)S(1)}, f32[1,1,4096]{2,1,0:T(1,128)S(1)}, u32[]{:S(2)}, u32[]{:S(2)}) collective-permute-start(f32[1,1,4096]{2,1,0:T(1,128)S(1)} %add.6.refs_0_), channel_id=1, source_target_pairs={{0,16},{8,24},{16,0},{24,8},{1,17},{9,25},{17,1},{25,9},{2,18},{10... | collective-permute-start | bytes 49160 | tf_op jit(solution)/shard_map/ppermute | solution.py:496
  33.8 4.2 %collective-permute-start.4 = (f32[1,1,4096]{2,1,0:T(1,128)S(1)}, f32[1,1,4096]{2,1,0:T(1,128)S(1)}, u32[]{:S(2)}, u32[]{:S(2)}) collective-permute-start(f32[1,1,4096]{2,1,0:T(1,128)S(1)} %add.6.refs_0_), channel_id=1, source_target_pairs={{0,8},{8,0},{16,24},{24,16},{1,9},{9,1},{17,25},{25,17},{2,10},{10... | collective-permute-start | bytes 49160 | tf_op jit(solution)/shard_map/ppermute | solution.py:496
  38.0 5.1 %collective-permute-start.9 = (f32[1,1,4096]{2,1,0:T(1,128)S(1)}, f32[1,1,4096]{2,1,0:T(1,128)S(1)}, u32[]{:S(2)}, u32[]{:S(2)}) collective-permute-start(f32[1,1,4096]{2,1,0:T(1,128)S(1)} %add.7.refs_0_), channel_id=1, source_target_pairs={{0,3},{1,2},{2,1},{3,0},{4,7},{5,6},{6,5},{7,4},{8,11},{9,10},{10,... | collective-permute-start | bytes 49160 | tf_op jit(solution)/shard_map/ppermute | solution.py:496
  40.9 5.2 %collective-permute-start.8 = (f32[1,1,4096]{2,1,0:T(1,128)S(1)}, f32[1,1,4096]{2,1,0:T(1,128)S(1)}, u32[]{:S(2)}, u32[]{:S(2)}) collective-permute-start(f32[1,1,4096]{2,1,0:T(1,128)S(1)} %add.7.refs_0_), channel_id=1, source_target_pairs={{0,2},{1,3},{2,0},{3,1},{4,6},{5,7},{6,4},{7,5},{8,10},{9,11},{10,... | collective-permute-start | bytes 49160 | tf_op jit(solution)/shard_map/ppermute | solution.py:496
  40.9 5.2 %collective-permute-start.7 = (f32[1,1,4096]{2,1,0:T(1,128)S(1)}, f32[1,1,4096]{2,1,0:T(1,128)S(1)}, u32[]{:S(2)}, u32[]{:S(2)}) collective-permute-start(f32[1,1,4096]{2,1,0:T(1,128)S(1)} %add.7.refs_0_), channel_id=1, source_target_pairs={{0,1},{1,0},{2,3},{3,2},{4,5},{5,4},{6,7},{7,6},{8,9},{9,8},{10,11... | collective-permute-start | bytes 49160 | tf_op jit(solution)/shard_map/ppermute | solution.py:496
  46.1 6.6 %collective-permute-start.10 = (f32[1,1,4096]{2,1,0:T(1,128)S(1)}, f32[1,1,4096]{2,1,0:T(1,128)S(1)}, u32[]{:S(2)}, u32[]{:S(2)}) collective-permute-start(f32[1,1,4096]{2,1,0:T(1,128)S(1)} %add.8.refs_0_), channel_id=1, source_target_pairs={{0,4},{1,5},{2,6},{3,7},{4,0},{5,1},{6,2},{7,3},{8,12},{9,13},{10,... | collective-permute-start | bytes 49160 | tf_op jit(solution)/shard_map/ppermute | solution.py:496
  52.7 42.8 %copy-start = (bf16[32,64,256]{2,1,0:T(8,128)(2,1)}, bf16[32,64,256]{2,1,0:T(8,128)(2,1)S(1)}, u32[]{:S(2)}) copy-start(bf16[32,64,256]{2,1,0:T(8,128)(2,1)S(1)} %all-to-all-done) | copy-start | bytes 3145732
